TPU v7x, 128 devices: a whole 4x4x4 slice. The times are simulated.
128 devices in a mesh: seq: 16 (over y_hi, z, core), tp: 8 (over y_lo, x).
Axes of the slice: x: 4, y: 4 (y_hi: 2, y_lo: 2; y = y_hi * 2 + y_lo), z: 4, core: 2. Of those that a mesh axis runs over, the one named last changes fastest.
Arguments:
- queries: bfloat16 [1024, 8192], P(None, 'tp'), may hold values from -80 to 80
- cache: bfloat16 [2, 16, 16384, 1024], P(None, None, 'seq', 'tp'), may hold values from -6 to 6
- draft_kv: bfloat16 [2, 1024, 1024], P(None, 'seq', 'tp'), may hold values from -9 to 9
- out_weight: bfloat16 [8192, 8192], P('tp', 'seq'), may hold values from -0.0625 to 0.0625
- lengths: int32 [16], replicated, may hold values from 1020 to 16376, as said below
- parents: int32 [16, 64], replicated, may hold values from -1 to 62, as said below
- path: int32 [16, 8], replicated, may hold values from 0 to 63, as said below
- accepted: int32 [16], replicated, may hold values from 1 to 8
Outputs:
- attn_out: bfloat16 [1024, 8192], P('tp', 'seq')
- new_cache: bfloat16 [2, 16, 16384, 1024], P(None, None, 'seq', 'tp')
Inputs may be any that keep to these rules, and one draw needn't show every extreme that they name: `lengths`: request r belongs to tenant t = r mod 4; a request of tenant t holds at most 16384 // 8 * 2 ** t - 8 tokens and at least half of that, and the first request of each tenant holds exactly that many. `parents`: node 0 is the root, with parent -1; every other node i has its parent among the nodes i - 7 to i - 1. `path`: for each request, the nodes of one branch of its tree, each the parent of the next, the last being node 63.
All inputs are finite; a program needn't handle non-finite values.
Results may differ from a plain program's by a relative error of at most 0.0051.
Values may be sent and summed in bfloat16 or wider, within the bound.
A program may use at most 192 MiB of HBM per device.

v0:
```python
import jax
import jax.numpy as jnp
from jax import lax
from jax.sharding import PartitionSpec as P

HEAD = 128
Q = 64
ACC = 8


masked_score = -1e30


def merged_2(array, axis, combine):
    everything = jax.tree.map(lambda part: lax.all_gather(part, axis), array)
    leading = jax.tree.map(lambda part: part[0], everything)

    def hop(k, so_far):
        return combine(so_far, jax.tree.map(lambda part: part[k], everything))

    return lax.fori_loop(1, lax.axis_size(axis), hop, leading)


def ancestors(parents):
    node_count = parents.shape[1]
    node_ids = jnp.arange(node_count, dtype=jnp.int32)
    step_map = (parents[:, :, None] == node_ids[None, None, :]).astype(jnp.float32)
    identity = jnp.broadcast_to(jnp.eye(node_count, dtype=jnp.float32), step_map.shape)
    reached = jnp.minimum(identity + step_map, 1.0)
    for doubling in range((node_count - 1).bit_length()):
        as_bits = reached.astype(jnp.bfloat16)
        squared = jnp.einsum("nij,njk->nik", as_bits, as_bits, preferred_element_type=jnp.float32)
        reached = jnp.minimum(squared, 1.0)
    return reached


def partial_block(query_rows, key_rows, value_rows, alive_mask):
    scores = jnp.einsum(
        "nqkge,npke->nqkgp", query_rows, key_rows, preferred_element_type=jnp.float32
    ) * HEAD ** (-0.5)
    masked = jnp.where(alive_mask, scores, masked_score)
    peak_score = jnp.max(masked, axis=-1)
    weights = jnp.where(alive_mask, jnp.exp(scores - peak_score[..., None]), 0.0)
    denominator = jnp.sum(weights, axis=-1)
    weighted = jnp.einsum(
        "nqkgp,npke->nqkge",
        weights.astype(jnp.bfloat16),
        value_rows,
        preferred_element_type=jnp.float32,
    )
    return (peak_score, denominator, weighted)


def join_flat(former, latter):
    peak_score = jnp.maximum(former[0], latter[0])
    weight_former = jnp.exp(former[0] - peak_score)
    weight_latter = jnp.exp(latter[0] - peak_score)
    row_count, head_count = peak_score.shape
    weighted = (
        former[2].reshape(row_count, head_count, -1) * weight_former[..., None]
        + latter[2].reshape(row_count, head_count, -1) * weight_latter[..., None]
    )
    return (
        peak_score,
        former[1] * weight_former + latter[1] * weight_latter,
        weighted.reshape(row_count, -1),
    )


def finish(query_flat, draft_rows, family, partials, kv_local):
    node_sets = family.shape[0]
    heads_local = query_flat.shape[1] // HEAD
    group_size = heads_local // kv_local
    reach = ancestors(family)
    query_rows = query_flat.reshape(node_sets, Q, kv_local, group_size, HEAD)
    key_rows = draft_rows[0].reshape(node_sets, Q, kv_local, HEAD)
    value_rows = draft_rows[1].reshape(node_sets, Q, kv_local, HEAD)
    draft_part = partial_block(query_rows, key_rows, value_rows, reach[:, :, None, None, :] > 0.5)
    row_count = node_sets * Q
    draft_part = (
        draft_part[0].reshape(row_count, heads_local),
        draft_part[1].reshape(row_count, heads_local),
        draft_part[2].reshape(row_count, heads_local * HEAD),
    )
    peak_score, denominator, weighted = join_flat(partials, draft_part)
    result = weighted.reshape(row_count, heads_local, HEAD) / denominator[..., None]
    return result.reshape(row_count, heads_local * HEAD).astype(jnp.bfloat16)


def select_rows(draft_rows, branch_path):
    node_sets = branch_path.shape[0]
    draft_table = draft_rows.reshape(2, node_sets, Q, draft_rows.shape[2])
    selector = (branch_path[:, :, None] == jnp.arange(Q, dtype=jnp.int32)[None, None, :]).astype(
        jnp.bfloat16
    )
    return jnp.einsum(
        "naq,xnqd->xnad", selector, draft_table, preferred_element_type=jnp.float32
    ).astype(jnp.bfloat16)


def local(queries, cache, draft_kv, out_weight, lengths, parents, path, accepted):
    seq_index = lax.axis_index("seq")
    requests = cache.shape[1]
    span_cache = cache.shape[2]
    kv_local = cache.shape[3] // HEAD
    heads_local = queries.shape[1] // HEAD
    group_size = heads_local // kv_local
    token_rows = requests * Q
    bundles = requests // 4
    positions = seq_index * span_cache + jnp.arange(span_cache, dtype=jnp.int32)
    alive_mask = positions[None, :] < lengths[:, None]
    query_blocks = queries.reshape(bundles, 4, Q, kv_local, group_size, HEAD)
    key_blocks = cache[0].reshape(bundles, 4, span_cache, kv_local, HEAD)
    value_blocks = cache[1].reshape(bundles, 4, span_cache, kv_local, HEAD)

    def cache_part(inputs):
        query_block, key_block, value_block, alive_block = inputs
        return partial_block(
            query_block, key_block, value_block, alive_block[:, None, None, None, :]
        )

    peak_score, denominator, weighted = lax.map(
        cache_part,
        (query_blocks, key_blocks, value_blocks, alive_mask.reshape(bundles, 4, span_cache)),
    )
    peak_score = peak_score.reshape(token_rows, heads_local)
    denominator = denominator.reshape(token_rows, heads_local)
    weighted = weighted.reshape(token_rows, heads_local * HEAD)
    drafts = lax.all_gather(draft_kv, "seq", axis=1, tiled=True)
    merged = merged_2((peak_score, denominator, weighted), "seq", join_flat)
    attended = finish(queries, drafts, parents, merged, kv_local)
    chosen = select_rows(drafts, path)
    attn_out = lax.psum_scatter(
        jnp.dot(attended, out_weight, preferred_element_type=jnp.float32),
        "tp",
        scatter_dimension=0,
        tiled=True,
    ).astype(jnp.bfloat16)
    offset = positions[None, :] - lengths[:, None]
    writable = (offset >= 0) & (offset < accepted[:, None])
    selector = (
        (offset[:, :, None] == jnp.arange(ACC, dtype=jnp.int32)[None, None, :])
        & writable[:, :, None]
    ).astype(jnp.bfloat16)
    placed = jnp.einsum(
        "rca,xrad->xrcd", selector, chosen, preferred_element_type=jnp.float32
    ).astype(jnp.bfloat16)
    new_cache = jnp.where(writable[None, :, :, None], placed, cache)
    return (attn_out, new_cache)


def solution(mesh):
    return jax.shard_map(
        local,
        mesh=mesh,
        in_specs=(
            P(None, "tp"),
            P(None, None, "seq", "tp"),
            P(None, "seq", "tp"),
            P("tp", "seq"),
            P(),
            P(),
            P(),
            P(),
        ),
        out_specs=(P("tp", "seq"), P(None, None, "seq", "tp")),
        check_vma=False,
    )
```

profile of v0, /device:TPU:114, one launch (start us, length us, event | category | flops | bytes accessed | tf_op | source)
XLA Modules:
  0.0 671.6 jit_solution(16713751382238479600)
XLA Ops:
  8.1 6.0 fusion.71
  14.8 38.0 %while.33 = (s32[]{:T(128)}, f32[4,4,64,1,8]{2,1,0,4,3:T(4,128)S(1)}, f32[4,4,64,1,8]{2,4,3,1,0:T(8,128)S(1)}, f32[4,4,64,1,8,128]{5,4,2,1,0,3:T(8,128)}, pred[4...) while((s32[]{:T(128)}, ...), condition=%wide.region_3.4_spmd, body=%wide.region_0.3_spmd.sunk | while | flops 1096806400 | bytes 32101996 | solution.py:122
  17.6 3.0 fusion.91
  36.6 3.0 fusion.91
  52.8 4.9 all_gather_reshape.11
  65.5 20.9 %all_gather.15 = bf16[2,1024,128]{2,1,0:T(8,128)(2,1)S(1)} all-gather(bf16[2,64,128]{2,1,0:T(8,128)(2,1)S(1)} %copy-done.7), channel_id=1, replica_groups=mesh['seq'=16,'tp'=8] {'seq'}, dimensions={1}, use_global_device_ids=true | all-gather | bytes 557056 | tf_op jit(solution)/shard_map/all_gather | solution.py:129
  95.4 26.0 %all_gather.13 = f32[16,1024,8]{1,2,0:T(8,128)S(1)} all-gather(f32[1,1024,8]{1,2,0:T(8,128)} %all_gather_reshape.10), channel_id=1, replica_groups=mesh['seq'=16,'tp'=8] {'seq'}, dimensions={0}, use_global_device_ids=true | all-gather | bytes 557056 | tf_op jit(solution)/shard_map/all_gather | solution.py:15
  121.4 23.3 %all_gather.12 = f32[16,1024,8]{1,2,0:T(8,128)S(1)} all-gather(f32[1,1024,8]{1,2,0:T(8,128)} %all_gather_reshape.9), channel_id=1, replica_groups=mesh['seq'=16,'tp'=8] {'seq'}, dimensions={0}, use_global_device_ids=true | all-gather | bytes 557056 | tf_op jit(solution)/shard_map/all_gather | solution.py:15
  144.7 4.3 fusion.73
  148.9 251.8 %all-gather.2.cloned.1.call-done = f32[16,1024,1024]{2,1,0:T(8,128)} async-done(((f32[1,1024,1024]{2,1,0:T(8,128)}), f32[16,1024,1024]{2,1,0:T(8,128)}) %all-gather.2.cloned.1.call-update) | async-done | bytes 67108880 | tf_op jit(solution)/shard_map/all_gather | solution.py:15
  400.8 4.8 slice_bitcast_fusion
  405.5 207.2 %while.34 = (s32[]{:T(128)}, f32[1024,8]{0,1:T(8,128)S(1)}, f32[1024,8]{0,1:T(8,128)S(1)}, f32[1024,1024]{1,0:T(8,128)}, f32[16,1024,8]{1,2,0:T(8,128)S(1)}, /*i...) while((s32[]{:T(128)}, f32[1024,8]{0,1:T(8,128)S(1)}, ...), condition=%wide.region_5.6_spmd, body=%wide.region_4.5_spmd.sunk | while | flops 3194885 | bytes 46596272 | solution.py:21
  410.7 8.6 %fusion.93 = f32[1024,1024]{1,0:T(8,128)} fusion(f32[128,8,8,128]{3,2,1,0:T(8,128)S(1)} %bitcast.239, f32[1024,1024]{1,0:T(8,128)} %get-tuple-element.461, f32[128,8,8,128]{3,2,1,0:T(8,128)S(1)} %bitcast.240, f32[16,1024,1024]{2,1,0:T(8,128)} %get-tuple-element.474, s32[]{:T(128)S(6)} %select_n.68), kind=kLoop, calls=%fused_computation.27.clone.1 | loop fusion | flops 3145728 | bytes 20971524 | tf_op jit(solution)/shard_map/while/body/eval_jaxpr/add | solution.py:60
  424.6 8.6 %fusion.93 = f32[1024,1024]{1,0:T(8,128)} fusion(f32[128,8,8,128]{3,2,1,0:T(8,128)S(1)} %bitcast.239, f32[1024,1024]{1,0:T(8,128)} %get-tuple-element.461, f32[128,8,8,128]{3,2,1,0:T(8,128)S(1)} %bitcast.240, f32[16,1024,1024]{2,1,0:T(8,128)} %get-tuple-element.474, s32[]{:T(128)S(6)} %select_n.68), kind=kLoop, calls=%fused_computation.27.clone.1 | loop fusion | flops 3145728 | bytes 20971524 | tf_op jit(solution)/shard_map/while/body/eval_jaxpr/add | solution.py:60
  438.4 8.6 %fusion.93 = f32[1024,1024]{1,0:T(8,128)} fusion(f32[128,8,8,128]{3,2,1,0:T(8,128)S(1)} %bitcast.239, f32[1024,1024]{1,0:T(8,128)} %get-tuple-element.461, f32[128,8,8,128]{3,2,1,0:T(8,128)S(1)} %bitcast.240, f32[16,1024,1024]{2,1,0:T(8,128)} %get-tuple-element.474, s32[]{:T(128)S(6)} %select_n.68), kind=kLoop, calls=%fused_computation.27.clone.1 | loop fusion | flops 3145728 | bytes 20971524 | tf_op jit(solution)/shard_map/while/body/eval_jaxpr/add | solution.py:60
  452.2 8.6 %fusion.93 = f32[1024,1024]{1,0:T(8,128)} fusion(f32[128,8,8,128]{3,2,1,0:T(8,128)S(1)} %bitcast.239, f32[1024,1024]{1,0:T(8,128)} %get-tuple-element.461, f32[128,8,8,128]{3,2,1,0:T(8,128)S(1)} %bitcast.240, f32[16,1024,1024]{2,1,0:T(8,128)} %get-tuple-element.474, s32[]{:T(128)S(6)} %select_n.68), kind=kLoop, calls=%fused_computation.27.clone.1 | loop fusion | flops 3145728 | bytes 20971524 | tf_op jit(solution)/shard_map/while/body/eval_jaxpr/add | solution.py:60
  466.0 8.6 %fusion.93 = f32[1024,1024]{1,0:T(8,128)} fusion(f32[128,8,8,128]{3,2,1,0:T(8,128)S(1)} %bitcast.239, f32[1024,1024]{1,0:T(8,128)} %get-tuple-element.461, f32[128,8,8,128]{3,2,1,0:T(8,128)S(1)} %bitcast.240, f32[16,1024,1024]{2,1,0:T(8,128)} %get-tuple-element.474, s32[]{:T(128)S(6)} %select_n.68), kind=kLoop, calls=%fused_computation.27.clone.1 | loop fusion | flops 3145728 | bytes 20971524 | tf_op jit(solution)/shard_map/while/body/eval_jaxpr/add | solution.py:60
  479.8 8.6 %fusion.93 = f32[1024,1024]{1,0:T(8,128)} fusion(f32[128,8,8,128]{3,2,1,0:T(8,128)S(1)} %bitcast.239, f32[1024,1024]{1,0:T(8,128)} %get-tuple-element.461, f32[128,8,8,128]{3,2,1,0:T(8,128)S(1)} %bitcast.240, f32[16,1024,1024]{2,1,0:T(8,128)} %get-tuple-element.474, s32[]{:T(128)S(6)} %select_n.68), kind=kLoop, calls=%fused_computation.27.clone.1 | loop fusion | flops 3145728 | bytes 20971524 | tf_op jit(solution)/shard_map/while/body/eval_jaxpr/add | solution.py:60
  493.6 8.6 %fusion.93 = f32[1024,1024]{1,0:T(8,128)} fusion(f32[128,8,8,128]{3,2,1,0:T(8,128)S(1)} %bitcast.239, f32[1024,1024]{1,0:T(8,128)} %get-tuple-element.461, f32[128,8,8,128]{3,2,1,0:T(8,128)S(1)} %bitcast.240, f32[16,1024,1024]{2,1,0:T(8,128)} %get-tuple-element.474, s32[]{:T(128)S(6)} %select_n.68), kind=kLoop, calls=%fused_computation.27.clone.1 | loop fusion | flops 3145728 | bytes 20971524 | tf_op jit(solution)/shard_map/while/body/eval_jaxpr/add | solution.py:60
  507.4 8.6 %fusion.93 = f32[1024,1024]{1,0:T(8,128)} fusion(f32[128,8,8,128]{3,2,1,0:T(8,128)S(1)} %bitcast.239, f32[1024,1024]{1,0:T(8,128)} %get-tuple-element.461, f32[128,8,8,128]{3,2,1,0:T(8,128)S(1)} %bitcast.240, f32[16,1024,1024]{2,1,0:T(8,128)} %get-tuple-element.474, s32[]{:T(128)S(6)} %select_n.68), kind=kLoop, calls=%fused_computation.27.clone.1 | loop fusion | flops 3145728 | bytes 20971524 | tf_op jit(solution)/shard_map/while/body/eval_jaxpr/add | solution.py:60
  521.2 8.6 %fusion.93 = f32[1024,1024]{1,0:T(8,128)} fusion(f32[128,8,8,128]{3,2,1,0:T(8,128)S(1)} %bitcast.239, f32[1024,1024]{1,0:T(8,128)} %get-tuple-element.461, f32[128,8,8,128]{3,2,1,0:T(8,128)S(1)} %bitcast.240, f32[16,1024,1024]{2,1,0:T(8,128)} %get-tuple-element.474, s32[]{:T(128)S(6)} %select_n.68), kind=kLoop, calls=%fused_computation.27.clone.1 | loop fusion | flops 3145728 | bytes 20971524 | tf_op jit(solution)/shard_map/while/body/eval_jaxpr/add | solution.py:60
  535.1 8.6 %fusion.93 = f32[1024,1024]{1,0:T(8,128)} fusion(f32[128,8,8,128]{3,2,1,0:T(8,128)S(1)} %bitcast.239, f32[1024,1024]{1,0:T(8,128)} %get-tuple-element.461, f32[128,8,8,128]{3,2,1,0:T(8,128)S(1)} %bitcast.240, f32[16,1024,1024]{2,1,0:T(8,128)} %get-tuple-element.474, s32[]{:T(128)S(6)} %select_n.68), kind=kLoop, calls=%fused_computation.27.clone.1 | loop fusion | flops 3145728 | bytes 20971524 | tf_op jit(solution)/shard_map/while/body/eval_jaxpr/add | solution.py:60
  548.9 8.6 %fusion.93 = f32[1024,1024]{1,0:T(8,128)} fusion(f32[128,8,8,128]{3,2,1,0:T(8,128)S(1)} %bitcast.239, f32[1024,1024]{1,0:T(8,128)} %get-tuple-element.461, f32[128,8,8,128]{3,2,1,0:T(8,128)S(1)} %bitcast.240, f32[16,1024,1024]{2,1,0:T(8,128)} %get-tuple-element.474, s32[]{:T(128)S(6)} %select_n.68), kind=kLoop, calls=%fused_computation.27.clone.1 | loop fusion | flops 3145728 | bytes 20971524 | tf_op jit(solution)/shard_map/while/body/eval_jaxpr/add | solution.py:60
  562.7 8.6 %fusion.93 = f32[1024,1024]{1,0:T(8,128)} fusion(f32[128,8,8,128]{3,2,1,0:T(8,128)S(1)} %bitcast.239, f32[1024,1024]{1,0:T(8,128)} %get-tuple-element.461, f32[128,8,8,128]{3,2,1,0:T(8,128)S(1)} %bitcast.240, f32[16,1024,1024]{2,1,0:T(8,128)} %get-tuple-element.474, s32[]{:T(128)S(6)} %select_n.68), kind=kLoop, calls=%fused_computation.27.clone.1 | loop fusion | flops 3145728 | bytes 20971524 | tf_op jit(solution)/shard_map/while/body/eval_jaxpr/add | solution.py:60
  576.5 8.6 %fusion.93 = f32[1024,1024]{1,0:T(8,128)} fusion(f32[128,8,8,128]{3,2,1,0:T(8,128)S(1)} %bitcast.239, f32[1024,1024]{1,0:T(8,128)} %get-tuple-element.461, f32[128,8,8,128]{3,2,1,0:T(8,128)S(1)} %bitcast.240, f32[16,1024,1024]{2,1,0:T(8,128)} %get-tuple-element.474, s32[]{:T(128)S(6)} %select_n.68), kind=kLoop, calls=%fused_computation.27.clone.1 | loop fusion | flops 3145728 | bytes 20971524 | tf_op jit(solution)/shard_map/while/body/eval_jaxpr/add | solution.py:60
  590.3 8.6 %fusion.93 = f32[1024,1024]{1,0:T(8,128)} fusion(f32[128,8,8,128]{3,2,1,0:T(8,128)S(1)} %bitcast.239, f32[1024,1024]{1,0:T(8,128)} %get-tuple-element.461, f32[128,8,8,128]{3,2,1,0:T(8,128)S(1)} %bitcast.240, f32[16,1024,1024]{2,1,0:T(8,128)} %get-tuple-element.474, s32[]{:T(128)S(6)} %select_n.68), kind=kLoop, calls=%fused_computation.27.clone.1 | loop fusion | flops 3145728 | bytes 20971524 | tf_op jit(solution)/shard_map/while/body/eval_jaxpr/add | solution.py:60
  604.1 8.6 %fusion.93 = f32[1024,1024]{1,0:T(8,128)} fusion(f32[128,8,8,128]{3,2,1,0:T(8,128)S(1)} %bitcast.239, f32[1024,1024]{1,0:T(8,128)} %get-tuple-element.461, f32[128,8,8,128]{3,2,1,0:T(8,128)S(1)} %bitcast.240, f32[16,1024,1024]{2,1,0:T(8,128)} %get-tuple-element.474, s32[]{:T(128)S(6)} %select_n.68), kind=kLoop, calls=%fused_computation.27.clone.1 | loop fusion | flops 3145728 | bytes 20971524 | tf_op jit(solution)/shard_map/while/body/eval_jaxpr/add | solution.py:60
  618.0 3.9 fusion.32
  621.9 12.3 %copy.77 = bf16[2,16,1024,128]{2,3,0,1:T(8,128)(2,1)} copy(bf16[2,16,1024,128]{3,2,1,0:T(8,128)(2,1)} %param.13) | data formatting | bytes 16777216 | tf_op args[1]
  634.5 7.1 %bitcast_select_fusion.1 = bf16[2,16,1024,128]{2,3,0,1:T(8,128)(2,1)} fusion(bf16[2,16,1024,128]{2,3,0,1:T(8,128)(2,1)} %copy.77, pred[16,1024]{1,0:T(8,128)(4,1)S(1)} %compare_and_fusion, bf16[2,16,64,128]{3,2,1,0:T(8,128)(2,1)S(1)} %bitcast.244, s32[16,1024]{1,0:T(8,128)S(1)} %broadcast_subtract_fusion, s32[16,8]{1,0:T(8,128)S(1)} %copy.75), kind=kOutput, calls=%fused_computation.35 | convolution fusion | flops 79994880 | bytes 17383936 | tf_op jit(solution)/shard_map/rca,xrad->xrcd/dot_general | solution.py:145
  641.6 11.9 %copy.78 = bf16[2,16,1024,128]{3,2,1,0:T(8,128)(2,1)} copy(bf16[2,16,1024,128]{2,3,0,1:T(8,128)(2,1)} %bitcast_select_fusion.1) | data formatting | bytes 16777216
  653.5 9.6 %reduce-scatter.2.cloned.1.call-done = f32[128,512]{1,0:T(8,128)} async-done(((f32[1024,512]{1,0:T(8,128)}), f32[128,512]{1,0:T(8,128)}) %reduce-scatter.2.cloned.1.call-update) | async-done | bytes 262160 | tf_op jit(solution)/shard_map/reduce_scatter | solution.py:133
  (197 shorter events, 134.6 us)
Async XLA Ops:
  7.2 609.7 %copy-start = (bf16[1024,512]{1,0:T(8,128)(2,1)S(1)}, bf16[1024,512]{1,0:T(8,128)(2,1)}, u32[]{:S(2)}) copy-start(bf16[1024,512]{1,0:T(8,128)(2,1)} %param.15) | copy-start | bytes 3145732
  7.2 393.6 %all-gather.2.cloned.1.call-start = ((), (), s32[]{:S(2)}) async-start(), calls=%async_computation.1 | async-start | bytes 71303168 | tf_op jit(solution)/shard_map/all_gather | solution.py:15
  8.1 6.0 copy-start.6
  57.7 1.6 copy-start.11
  57.7 7.8 %copy-start.7 = (bf16[2,64,128]{2,1,0:T(8,128)(2,1)S(1)}, bf16[2,64,128]{2,1,0:T(8,128)(2,1)}, u32[]{:S(2)}) copy-start(bf16[2,64,128]{2,1,0:T(8,128)(2,1)} %param.14) | copy-start | bytes 98308
  57.7 605.4 %reduce-scatter.2.cloned.1.call-start = ((), (), s32[]{:S(2)}) async-start(), calls=%async_computation.2 | async-start | bytes 2359296 | tf_op jit(solution)/shard_map/reduce_scatter | solution.py:133
  86.4 0.8 copy-start.3
  408.5 2.2 copy-start.1
  422.4 2.2 copy-start.1
  436.2 2.2 copy-start.1
  450.0 2.2 copy-start.1
  463.8 2.2 copy-start.1
  477.6 2.2 copy-start.1
  491.4 2.2 copy-start.1
  505.2 2.2 copy-start.1
  519.1 2.2 copy-start.1
  532.9 2.2 copy-start.1
  546.7 2.2 copy-start.1
  560.5 2.2 copy-start.1
  574.3 2.2 copy-start.1
  588.1 2.2 copy-start.1
  601.9 2.2 copy-start.1
  614.5 2.3 copy-start.2
  614.5 3.5 copy-start.5
  621.9 12.4 %copy-start.9 = (s32[16,8]{0,1:T(8,128)S(1)}, s32[16,8]{0,1:T(8,128)}, u32[]{:S(2)}) copy-start(s32[16,8]{0,1:T(8,128)} %param.18) | copy-start | bytes 1540
  621.9 12.4 %copy-start.8 = (s32[16]{0:T(128)S(1)}, s32[16]{0:T(128)}, u32[]{:S(2)}) copy-start(s32[16]{0:T(128)} %param.16) | copy-start | bytes 196
  621.9 12.4 %copy-start.10 = (s32[16]{0:T(128)S(1)}, s32[16]{0:T(128)}, u32[]{:S(2)}) copy-start(s32[16]{0:T(128)} %param.19) | copy-start | bytes 196
  621.9 12.6 %copy-start.4 = (bf16[2,1024,128]{2,1,0:T(8,128)(2,1)S(1)}, bf16[2,1024,128]{2,1,0:T(8,128)(2,1)}, u32[]{:S(2)}) copy-start(bf16[2,1024,128]{2,1,0:T(8,128)(2,1)} %copy-done.3) | copy-start | bytes 1572868
Sparse Core Ops, SparseCore 0:
  57.8 342.8 all-gather.1
  622.0 41.0 reduce-scatter.1
where the time goes:
time: 678 us; the launch traced here: 672 us
  waiting for transfers between devices  261 us (38%)
  other arithmetic  141 us (21%)
  local copies, waits for them, and re-layouts  137 us (20%)
  blocking collectives  70.2 us (10%)
  matrix products  46.2 us (7%)
  between operations  14.3 us (2%)
    all_gather x1, waiting for transfers between devices, merged_2(): everything = jax.tree.map(lambda part: lax.all_gather(part, axis), array)  252 us
    add x15, other arithmetic, join_flat(): former[2].reshape(row_count, head_count, -1) * weight_former[..., None]  129 us
    all_gather x2, blocking collectives, merged_2(): everything = jax.tree.map(lambda part: lax.all_gather(part, axis), array)  49.3 us
    mul x16, local copies, waits for them, and re-layouts, join_flat(): latter[2].reshape(row_count, head_count, -1) * weight_latter[..., None]  39.8 us
    unnamed x26, local copies, waits for them, and re-layouts  26.8 us
    all_gather x1, blocking collectives, local(): drafts = lax.all_gather(draft_kv, 'seq', axis=1, tiled=True)  20.9 us
    mul x16, local copies, waits for them, and re-layouts, join_flat(): former[2].reshape(row_count, head_count, -1) * weight_former[..., None]  18.2 us
    dot_general x5, matrix products, partial_block(): jnp.einsum('nqkgp,npke->nqkge', weights.astype(jnp.bfloat16), value_rows,...  16.4 us
  transfers between devices with their start and end apart: 2, of which 2 were waited for; matrix products, arithmetic and copies ran while one was open for 8% of the time, Pallas kernels for 0%

commit v1 on v0

v1 whole, which is shorter than its diff:
```python
import functools

import jax
import jax.numpy as jnp
from jax import lax
from jax.experimental import pallas as pl
from jax.experimental.pallas import tpu as pltpu
from jax.sharding import PartitionSpec as P

HEAD = 128
Q = 64
ACC = 8
MESH = pl.DeviceIdType.MESH
SCALE = HEAD**-0.5 * 1.4426950408889634
DEAD = -1e30
CHUNK = 256
WINDOW = 32


def stacked_heads(rows):
    heads = rows.shape[1] // HEAD
    return jnp.concatenate([rows[:, h * HEAD : (h + 1) * HEAD] for h in range(heads)], axis=0)


def attend_kernel(len_ref, q_ref, kv_ref, o_ref, st_ref, nc_ref, s_ref, acc_ref, max_ref, sem):
    span = kv_ref.shape[2]
    chunks = span // CHUNK
    width = s_ref.shape[1]
    r = pl.program_id(0)
    live = jnp.clip(len_ref[r] - lax.axis_index("seq") * span, 0, span)
    copy = pltpu.make_async_copy(kv_ref, nc_ref.at[:, pl.ds(r, 1)], sem)
    copy.start()

    def scores(at):
        return lax.dot_general(
            kv_ref[0, 0, pl.ds(at, CHUNK), :],
            stacked_heads(q_ref[...]),
            (((1,), (1,)), ((), ())),
            preferred_element_type=jnp.float32,
        )

    def folded(s):
        return jnp.max(s.reshape(CHUNK // 8, 8, width), axis=0)

    def weighted(at, p):
        values = kv_ref[1, 0, pl.ds(at, CHUNK), :].T
        values = jnp.concatenate([values, jnp.ones((16, CHUNK), values.dtype)], axis=0)
        return jnp.dot(values, p, preferred_element_type=jnp.float32)

    def publish(peak, acc):
        o_ref[0] = acc[:HEAD].astype(o_ref.dtype)
        st_ref[0, 0:1] = peak
        st_ref[0, 1:2] = acc[HEAD : HEAD + 1]

    @pl.when(live == 0)
    def _():
        publish(jnp.full((1, width), DEAD, jnp.float32), jnp.zeros((HEAD + 16, width), jnp.float32))

    @pl.when(live == span)
    def _():
        peak = None
        for c in range(chunks):
            s = scores(c * CHUNK)
            s_ref[pl.ds(c * CHUNK, CHUNK), :] = s
            peak = folded(s) if peak is None else jnp.maximum(peak, folded(s))
        peak = jnp.max(peak, axis=0, keepdims=True) * SCALE
        acc = None
        for c in range(chunks):
            p = jnp.exp2(s_ref[pl.ds(c * CHUNK, CHUNK), :] * SCALE - peak).astype(jnp.bfloat16)
            term = weighted(c * CHUNK, p)
            acc = term if acc is None else acc + term
        publish(peak, acc)

    @pl.when((live > 0) & (live < span))
    def _():
        used = (live + CHUNK - 1) // CHUNK
        max_ref[...] = jnp.full_like(max_ref, DEAD)
        acc_ref[...] = jnp.zeros_like(acc_ref)

        def first(c, _):
            at = pl.multiple_of(c * CHUNK, CHUNK)
            row = lax.broadcasted_iota(jnp.int32, (CHUNK, width), 0) + at
            s = jnp.where(row < live, scores(at), DEAD)
            s_ref[pl.ds(at, CHUNK), :] = s
            max_ref[...] = jnp.maximum(max_ref[...], folded(s))
            return 0

        lax.fori_loop(0, used, first, 0)
        peak = jnp.max(max_ref[...], axis=0, keepdims=True) * SCALE

        def second(c, _):
            at = pl.multiple_of(c * CHUNK, CHUNK)
            row = lax.broadcasted_iota(jnp.int32, (CHUNK, width), 0) + at
            p = jnp.exp2(s_ref[pl.ds(at, CHUNK), :] * SCALE - peak)
            p = jnp.where(row < live, p, 0.0).astype(jnp.bfloat16)
            acc_ref[...] += weighted(at, p)
            return 0

        lax.fori_loop(0, used, second, 0)
        publish(peak, acc_ref[...])

    copy.wait()


def attend(lengths, queries, cache):
    requests, span = cache.shape[1], cache.shape[2]
    width = queries.shape[1] // HEAD * Q
    return pl.pallas_call(
        attend_kernel,
        out_shape=(
            jax.ShapeDtypeStruct((requests, HEAD, width), jnp.bfloat16),
            jax.ShapeDtypeStruct((requests, 8, width), jnp.float32),
            jax.ShapeDtypeStruct(cache.shape, cache.dtype),
        ),
        grid_spec=pltpu.PrefetchScalarGridSpec(
            num_scalar_prefetch=1,
            grid=(requests,),
            in_specs=[
                pl.BlockSpec((Q, queries.shape[1]), lambda r, n: (r, 0)),
                pl.BlockSpec((2, 1, span, HEAD), lambda r, n: (0, r, 0, 0)),
            ],
            out_specs=(
                pl.BlockSpec((1, HEAD, width), lambda r, n: (r, 0, 0)),
                pl.BlockSpec((1, 8, width), lambda r, n: (r, 0, 0)),
                pl.BlockSpec(memory_space=pl.ANY),
            ),
            scratch_shapes=[
                pltpu.VMEM((span, width), jnp.float32),
                pltpu.VMEM((HEAD + 16, width), jnp.float32),
                pltpu.VMEM((8, width), jnp.float32),
                pltpu.SemaphoreType.DMA,
            ],
        ),
        compiler_params=pltpu.CompilerParams(vmem_limit_bytes=32 << 20),
        name="attend",
    )(lengths, queries, cache)


def commit_kernel(len_ref, path_ref, acc_ref, draft_ref, nc_in, nc_ref, win_ref, load_sem, store_sem):
    requests, span = nc_ref.shape[1], nc_ref.shape[2]
    base = lax.axis_index("seq") * span

    def place(r):
        off = len_ref[r] - base
        hit = (off + acc_ref[r] > 0) & (off < span)
        start = pl.multiple_of(jnp.clip(off // 16 * 16, 0, span - WINDOW), 16)
        return off, hit, start

    def load(r, start):
        return pltpu.make_async_copy(
            nc_ref.at[:, r, pl.ds(start, WINDOW), :], win_ref.at[r], load_sem.at[r]
        )

    def store(r, start):
        return pltpu.make_async_copy(
            win_ref.at[r], nc_ref.at[:, r, pl.ds(start, WINDOW), :], store_sem.at[r]
        )

    def begin(r, _):
        off, hit, start = place(r)

        @pl.when(hit)
        def _():
            load(r, start).start()

        return 0

    def change(r, _):
        off, hit, start = place(r)

        @pl.when(hit)
        def _():
            row = lax.broadcasted_iota(jnp.int32, (WINDOW, Q), 0) + (start - off)
            node = lax.broadcasted_iota(jnp.int32, (WINDOW, Q), 1)
            pick = jnp.zeros((WINDOW, Q), jnp.float32)
            for j in range(ACC):
                pick = jnp.where((row == j) & (node == path_ref[r, j]), 1.0, pick)
            slot = lax.broadcasted_iota(jnp.int32, (WINDOW, HEAD), 0) + (start - off)
            fresh = (slot >= 0) & (slot < acc_ref[r])
            load(r, start).wait()
            for x in range(2):
                rows = jnp.dot(
                    pick.astype(jnp.bfloat16),
                    draft_ref[x, pl.ds(pl.multiple_of(r * Q, Q), Q), :],
                    preferred_element_type=jnp.float32,
                )
                old = win_ref[r, x].astype(jnp.float32)
                win_ref[r, x] = jnp.where(fresh, rows, old).astype(jnp.bfloat16)
            store(r, start).start()

        return 0

    def end(r, _):
        off, hit, start = place(r)

        @pl.when(hit)
        def _():
            store(r, start).wait()

        return 0

    lax.fori_loop(0, requests, begin, 0)
    lax.fori_loop(0, requests, change, 0)
    lax.fori_loop(0, requests, end, 0)


def commit(lengths, path, accepted, drafts, new_cache):
    requests = new_cache.shape[1]
    return pl.pallas_call(
        commit_kernel,
        out_shape=jax.ShapeDtypeStruct(new_cache.shape, new_cache.dtype),
        in_specs=[pl.BlockSpec(memory_space=pltpu.SMEM)] * 3
        + [pl.BlockSpec(memory_space=pltpu.VMEM), pl.BlockSpec(memory_space=pl.ANY)],
        out_specs=pl.BlockSpec(memory_space=pl.ANY),
        scratch_shapes=[
            pltpu.VMEM((requests, 2, WINDOW, HEAD), jnp.bfloat16),
            pltpu.SemaphoreType.DMA((requests,)),
            pltpu.SemaphoreType.DMA((requests,)),
        ],
        input_output_aliases={4: 0},
        name="commit",
    )(lengths, path, accepted, drafts, new_cache)


def closure(parents):
    nodes = jnp.arange(Q, dtype=jnp.int32)
    reached = ((parents[:, None] == nodes[None, :]) | (nodes[:, None] == nodes[None, :])).astype(jnp.bfloat16)
    for _ in range((Q - 1).bit_length()):
        reached = jnp.minimum(jnp.dot(reached, reached, preferred_element_type=jnp.float32), 1.0).astype(jnp.bfloat16)
    return reached


def local(queries, cache, draft_kv, out_weight, lengths, parents, path, accepted):
    s = lax.axis_index("seq")
    drafts = lax.all_gather(draft_kv, "seq", axis=1, tiled=True)
    o, st, new_cache = attend(lengths, queries, cache)
    m, l = st[:, 0, :], st[:, 1, :]
    reach = closure(lax.dynamic_index_in_dim(parents, s, 0, False))
    q = stacked_heads(lax.dynamic_slice_in_dim(queries, s * Q, Q, 0))
    ds = lax.dot_general(draft_kv[0], q, (((1,), (1,)), ((), ())), preferred_element_type=jnp.float32)
    ok = jnp.tile(reach.T, (1, q.shape[0] // Q)) > 0.5
    ds = jnp.where(ok, ds, DEAD)
    dm = jnp.max(ds, axis=0) * SCALE
    dp = jnp.where(ok, jnp.exp2(ds * SCALE - dm), 0.0)
    dl = jnp.sum(dp, axis=0)
    do = lax.dot_general(draft_kv[1], dp.astype(jnp.bfloat16), (((0,), (0,)), ((), ())), preferred_element_type=jnp.float32)
    mine = jnp.arange(m.shape[0]) == s
    top = lax.pmax(jnp.maximum(m, jnp.where(mine[:, None], dm[None], DEAD)), "seq")
    f = jnp.exp2(m - top)
    df = jnp.where(mine[:, None], jnp.exp2(dm[None] - top), 0.0)
    total = lax.psum(l * f + dl[None] * df, "seq")
    part = (o.astype(jnp.float32) * f[:, None, :] + do[None] * df[:, None, :]) / total[:, None, :]
    one = lax.psum_scatter(part, "seq", scatter_dimension=0, tiled=True)[0].astype(jnp.bfloat16)
    heads = one.shape[1] // Q
    one = one.reshape(HEAD, heads, Q).transpose(2, 1, 0).reshape(Q, heads * HEAD)
    attended = lax.all_gather(one, "seq", axis=0, tiled=True)
    attn_out = lax.psum_scatter(
        jnp.dot(attended, out_weight, preferred_element_type=jnp.float32), "tp", scatter_dimension=0, tiled=True
    ).astype(jnp.bfloat16)
    return attn_out, commit(lengths, path, accepted, drafts, new_cache)


def solution(mesh):
    return jax.shard_map(
        local,
        mesh=mesh,
        in_specs=(
            P(None, "tp"),
            P(None, None, "seq", "tp"),
            P(None, "seq", "tp"),
            P("tp", "seq"),
            P(),
            P(),
            P(),
            P(),
        ),
        out_specs=(P("tp", "seq"), P(None, None, "seq", "tp")),
        check_vma=False,
    )
```

time: 678 us -> 365 us (0.54)
  other arithmetic: 141 us -> 7.64 us
  local copies, waits for them, and re-layouts: 137 us -> 16.5 us
  waiting for transfers between devices: 261 us -> 149 us
  blocking collectives: 70.2 us -> 148 us
  matrix products: 46.2 us -> 7.63 us
  Pallas kernels: 0 us -> 16.1 us
    all_gather x1, waiting for transfers between devices: 252 us -> 48 us  [local(): attended = lax.all_gather(one, 'seq', axis=0, tiled=True)]
    add x32 -> x1, other arithmetic: 130 us -> 1.45 us  [local(): total = lax.psum(l * f + dl[None] * df, 'seq')]
    reduce_scatter x0 -> x1, waiting for transfers between devices: none -> 84.4 us  [local(): lax.psum_scatter(part, 'seq', scatter_dimension=0, tiled=True)[0]]
    psum x0 -> x1, blocking collectives: none -> 65.5 us  [local(): total = lax.psum(l * f + dl[None] * df, 'seq')]
    pmax x0 -> x1, blocking collectives: none -> 61.4 us  [local(): lax.pmax(jnp.maximum(m, jnp.where(mine[:, None], dm[None], DEAD)), 'seq')]
    mul x32 -> x0, local copies, waits for them, and re-layouts: 58 us -> none  [the longest x16 39.8 us: join_flat(): latter[2].reshape(row_count, head_count, -1) * weight_latter[..., None]]
    all_gather x2 -> x0, blocking collectives: 49.3 us -> none  [merged_2(): everything = jax.tree.map(lambda part: lax.all_gather(part, axis), array)]
    dot_general x14 -> x5, matrix products: 42.4 us -> 3.45 us  [the longest x1 1.65 us: local(): lax.dot_general(draft_kv[1], dp.astype(jnp.bfloat16), (((0,), (0,)), ((),...]
  transfers between devices with their start and end apart: 2 -> 3, of which waited for: 2 -> 3; matrix products, arithmetic and copies ran while one was open for 8% -> 0% of each run, Pallas kernels for 0% -> 1%
where the time goes in v1:
time: 365 us; the launch traced here: 359 us
  waiting for transfers between devices  149 us (41%)
  blocking collectives  148 us (41%)
  local copies, waits for them, and re-layouts  16.5 us (5%)
  Pallas kernels  16.1 us (4%)
  between operations  13.9 us (4%)
  other arithmetic  7.64 us (2%)
  matrix products  7.63 us (2%)
    reduce_scatter x1, waiting for transfers between devices, local(): lax.psum_scatter(part, 'seq', scatter_dimension=0, tiled=True)[0]  84.4 us
    psum x1, blocking collectives, local(): total = lax.psum(l * f + dl[None] * df, 'seq')  65.5 us
    pmax x1, blocking collectives, local(): lax.pmax(jnp.maximum(m, jnp.where(mine[:, None], dm[None], DEAD)), 'seq')  61.4 us
    all_gather x1, waiting for transfers between devices, local(): attended = lax.all_gather(one, 'seq', axis=0, tiled=True)  48 us
    all_gather x1, blocking collectives, local(): drafts = lax.all_gather(draft_kv, 'seq', axis=1, tiled=True)  21.3 us
    reduce_scatter x1, waiting for transfers between devices, local(): lax.psum_scatter(jnp.dot(attended, out_weight, preferred_element_type=jnp...  16.4 us
    pallas_call x1, Pallas kernels, attend(): pl.pallas_call(attend_kernel, out_shape=(jax.ShapeDtypeStruct((requests,...  14.1 us
    unnamed x20, local copies, waits for them, and re-layouts  12 us
  transfers between devices with their start and end apart: 3, of which 3 were waited for; matrix products, arithmetic and copies ran while one was open for 0% of the time, Pallas kernels for 1%

profile of v1, /device:TPU:114, one launch (start us, length us, event | category | flops | bytes accessed | tf_op | source)
XLA Modules:
  0.0 359.1 jit_solution(11370367497739131192)
XLA Ops:
  7.2 0.8 dynamic-slice_bitcast_fusion
  9.2 0.7 constant_dynamic-update-slice_fusion.7
  9.9 0.7 constant_dynamic-update-slice_fusion.6
  10.6 0.7 constant_dynamic-update-slice_fusion.5
  11.3 0.7 constant_dynamic-update-slice_fusion.4
  12.1 0.7 constant_dynamic-update-slice_fusion.3
  12.8 0.7 constant_dynamic-update-slice_fusion.2
  13.5 0.7 constant_dynamic-update-slice_fusion.1
  14.2 0.7 constant_dynamic-update-slice_fusion
  15.0 0.9 fusion.34
  15.9 1.6 convolution_bitcast_fusion
  17.6 3.4 copy-done.1
  21.0 1.6 copy-done.2
  23.2 14.1 %attend.1 = (bf16[16,128,512]{2,1,0:T(8,128)(2,1)S(1)}, f32[16,8,512]{2,1,0:T(8,128)S(1)}, bf16[2,16,1024,128]{3,2,1,0:T(8,128)(2,1)}) custom-call(s32[16]{0:T(128)S(1)} %copy-done.3, bf16[1024,1024]{1,0:T(8,128)(2,1)S(1)} %copy-done.2, bf16[2,16,1024,128]{3,2,1,0:T(8,128)(2,1)S(1)} %copy-done.1), custom_call_target="tpu_custom_call" | custom-call | tf_op jit(solution)/shard_map/attend/pallas_call | solution.py:108
  37.3 0.8 copy.14
  38.2 1.1 copy.15
  39.2 0.8 select_maximum_fusion
  40.1 61.4 %pmax.7 = f32[16,512]{1,0:T(8,128)S(1)} all-reduce(f32[16,512]{1,0:T(8,128)S(1)} %select_maximum_fusion), channel_id=1, replica_groups=mesh['seq'=16,'tp'=8] {'seq'}, use_global_device_ids=true, to_apply=%region_1.2 | all-reduce | flops 8192 | bytes 65536 | tf_op jit(solution)/shard_map/pmax | solution.py:248
  101.5 1.4 fusion.15
  102.9 65.5 %psum.7 = f32[16,512]{1,0:T(8,128)S(1)} all-reduce(f32[16,512]{1,0:T(8,128)} %get-tuple-element.8), channel_id=1, replica_groups=mesh['seq'=16,'tp'=8] {'seq'}, use_global_device_ids=true, to_apply=%region_3.4 | all-reduce | flops 8192 | bytes 65536 | tf_op jit(solution)/shard_map/psum | solution.py:251
  168.4 2.7 add_divide_fusion
  171.2 84.4 %reduce-scatter.3.cloned.1.call-done = f32[1,128,512]{2,1,0:T(8,128)} async-done(((f32[16,128,512]{2,1,0:T(8,128)}), f32[1,128,512]{2,1,0:T(8,128)}) %reduce-scatter.3.cloned.1.call-update) | async-done | bytes 262160 | tf_op jit(solution)/shard_map/reduce_scatter | solution.py:253
  255.7 1.0 convert_element_type.44
  256.8 0.7 copy.23
  257.5 48.0 %all-gather.2.cloned.1.call-done = bf16[1024,1024]{1,0:T(8,128)(2,1)} async-done(((bf16[64,1024]{1,0:T(8,128)(2,1)}), bf16[1024,1024]{1,0:T(8,128)(2,1)}) %all-gather.2.cloned.1.call-update) | async-done | bytes 2097168 | tf_op jit(solution)/shard_map/all_gather | solution.py:256
  305.6 4.2 %fusion.35 = f32[1024,512]{1,0:T(8,128)} fusion(bf16[1024,1024]{1,0:T(8,128)(2,1)} %all-gather.2.cloned.1.call-done, bf16[1024,512]{1,0:T(8,128)(2,1)S(1)} %copy-done), kind=kOutput, calls=%fused_computation.60 | convolution fusion | flops 1073741824 | bytes 5242880 | tf_op jit(solution)/shard_map/dot_general | solution.py:258
  309.8 0.7 copy-done.5
  310.4 0.7 copy.18.path_ref
  311.1 21.3 %all_gather.7.draft_ref = bf16[2,1024,128]{2,1,0:T(8,128)(2,1)} all-gather(bf16[2,64,128]{2,1,0:T(8,128)(2,1)S(1)} %copy-done.4), channel_id=1, replica_groups=mesh['seq'=16,'tp'=8] {'seq'}, dimensions={1}, use_global_device_ids=true | all-gather | bytes 557056 | tf_op jit(solution)/shard_map/all_gather | solution.py:235
  332.4 2.1 commit.1
  334.5 16.4 %reduce-scatter.5.cloned.1.call-done = f32[128,512]{1,0:T(8,128)} async-done(((f32[1024,512]{1,0:T(8,128)}), f32[128,512]{1,0:T(8,128)}) %reduce-scatter.5.cloned.1.call-update) | async-done | bytes 262160 | tf_op jit(solution)/shard_map/reduce_scatter | solution.py:257
  350.9 1.6 convert_element_type.46
  (25 shorter events, 2.2 us)
Async XLA Ops:
  7.2 298.4 %copy-start = (bf16[1024,512]{1,0:T(8,128)(2,1)S(1)}, bf16[1024,512]{1,0:T(8,128)(2,1)}, u32[]{:S(2)}) copy-start(bf16[1024,512]{1,0:T(8,128)(2,1)} %param.11) | copy-start | bytes 3145732
  7.2 248.5 %reduce-scatter.3.cloned.1.call-start = ((), (), s32[]{:S(2)}) async-start(), calls=%async_computation.2 | async-start | bytes 4456448 | tf_op jit(solution)/shard_map/reduce_scatter | solution.py:253
  17.6 3.4 copy-start.1
  21.0 1.6 copy-start.2
  22.6 0.7 copy-start.3
  171.2 134.4 %all-gather.2.cloned.1.call-start = ((), (), s32[]{:S(2)}) async-start(), calls=%async_computation.3 | async-start | bytes 2228224 | tf_op jit(solution)/shard_map/all_gather | solution.py:256
  257.5 93.5 %reduce-scatter.5.cloned.1.call-start = ((), (), s32[]{:S(2)}) async-start(), calls=%async_computation.4 | async-start | bytes 2359296 | tf_op jit(solution)/shard_map/reduce_scatter | solution.py:257
  309.7 0.7 copy-start.5
  309.7 1.4 copy-start.4
Sparse Core Ops, SparseCore 0:
  171.3 84.3 reduce-scatter.2
  259.0 46.4 all-gather.1
  309.9 41.0 reduce-scatter.4

commit v2 on v1

--- a/solution.py
+++ b/solution.py
@@ -131,12 +131,14 @@
                 pltpu.SemaphoreType.DMA,
             ],
         ),
-        compiler_params=pltpu.CompilerParams(vmem_limit_bytes=32 << 20),
+        compiler_params=pltpu.CompilerParams(vmem_limit_bytes=56 << 20),
         name="attend",
     )(lengths, queries, cache)
 
 
-def commit_kernel(len_ref, path_ref, acc_ref, draft_ref, nc_in, nc_ref, win_ref, load_sem, store_sem):
+def commit_kernel(
+    len_ref, path_ref, acc_ref, draft_ref, attn_ref, nc_in, out_ref, nc_ref, win_ref, load_sem, store_sem
+):
     requests, span = nc_ref.shape[1], nc_ref.shape[2]
     base = lax.axis_index("seq") * span
 
@@ -200,67 +202,323 @@
         return 0
 
     lax.fori_loop(0, requests, begin, 0)
+    out_ref[...] = attn_ref[...]
     lax.fori_loop(0, requests, change, 0)
     lax.fori_loop(0, requests, end, 0)
 
 
-def commit(lengths, path, accepted, drafts, new_cache):
+def commit(lengths, path, accepted, drafts, attn, new_cache):
     requests = new_cache.shape[1]
     return pl.pallas_call(
         commit_kernel,
-        out_shape=jax.ShapeDtypeStruct(new_cache.shape, new_cache.dtype),
+        out_shape=(
+            jax.ShapeDtypeStruct(attn.shape, attn.dtype),
+            jax.ShapeDtypeStruct(new_cache.shape, new_cache.dtype),
+        ),
         in_specs=[pl.BlockSpec(memory_space=pltpu.SMEM)] * 3
-        + [pl.BlockSpec(memory_space=pltpu.VMEM), pl.BlockSpec(memory_space=pl.ANY)],
-        out_specs=pl.BlockSpec(memory_space=pl.ANY),
+        + [pl.BlockSpec(memory_space=pltpu.VMEM)] * 2
+        + [pl.BlockSpec(memory_space=pl.ANY)],
+        out_specs=(pl.BlockSpec(memory_space=pltpu.VMEM), pl.BlockSpec(memory_space=pl.ANY)),
         scratch_shapes=[
             pltpu.VMEM((requests, 2, WINDOW, HEAD), jnp.bfloat16),
             pltpu.SemaphoreType.DMA((requests,)),
             pltpu.SemaphoreType.DMA((requests,)),
         ],
-        input_output_aliases={4: 0},
+        input_output_aliases={5: 1},
         name="commit",
-    )(lengths, path, accepted, drafts, new_cache)
-
-
-def closure(parents):
-    nodes = jnp.arange(Q, dtype=jnp.int32)
-    reached = ((parents[:, None] == nodes[None, :]) | (nodes[:, None] == nodes[None, :])).astype(jnp.bfloat16)
+    )(lengths, path, accepted, drafts, attn, new_cache)
+
+
+def folded_parts(first, second):
+    peak = jnp.maximum(first[0], second[0])
+    a, b = jnp.exp2(first[0] - peak), jnp.exp2(second[0] - peak)
+    return peak, first[1] * a + second[1] * b, a, b
+
+
+def join_kernel(
+    o_ref, st_ref, q_hbm, dkv_ref, par_ref, w_ref, out_ref,
+    q_ref, pair_o, pair_st, merge_o, merge_st, acc_ref, run_ref, att, rs_send, rs_recv,
+    q_sem, pair_ss, pair_rs, merge_ss, merge_rs, own_ss, relay_ss, pass_ss, att_rs, out_ss, out_rs,
+):
+    s, t = lax.axis_index("seq"), lax.axis_index("tp")
+    k, c = s // 2, s % 2
+    y, z = k // 4, k % 4
+    chips, tps = pair_o.shape[0], rs_send.shape[0]
+    partner = 2 * k + 1 - c
+    width = o_ref.shape[2]
+    heads = width // Q
+
+    barrier = pltpu.get_barrier_semaphore()
+    for d in range(1, chips):
+        pl.semaphore_signal(barrier, inc=1, device_id={"seq": 2 * ((k + d) % chips) + c}, device_id_type=MESH)
+    pl.semaphore_signal(barrier, inc=1, device_id={"seq": partner}, device_id_type=MESH)
+    for d in range(1, tps):
+        pl.semaphore_signal(barrier, inc=1, device_id={"tp": (t + d) % tps}, device_id_type=MESH)
+    q_copy = pltpu.make_async_copy(q_hbm.at[pl.ds(pl.multiple_of(s * Q, Q), Q), :], q_ref, q_sem)
+    q_copy.start()
+    pl.semaphore_wait(barrier, chips + tps - 1)
+
+    def send(src, dst, ss, rs, **where):
+        return pltpu.make_async_remote_copy(
+            src_ref=src, dst_ref=dst, send_sem=ss, recv_sem=rs, device_id=where, device_id_type=MESH
+        )
+
+    def pair_copies(j):
+        r = 2 * j + 1 - c
+        return (
+            send(o_ref.at[r], pair_o.at[j], pair_ss.at[j, 0], pair_rs.at[j, 0], seq=partner),
+            send(st_ref.at[r], pair_st.at[j], pair_ss.at[j, 1], pair_rs.at[j, 1], seq=partner),
+        )
+
+    def merge_copies(j):
+        return (
+            send(pair_o.at[j], merge_o.at[k], merge_ss.at[j, 0], merge_rs.at[k, 0], seq=2 * j + c),
+            send(pair_st.at[j], merge_st.at[k], merge_ss.at[j, 1], merge_rs.at[k, 1], seq=2 * j + c),
+        )
+
+    def merge_arrival(i):
+        return (
+            send(pair_o.at[i], merge_o.at[i], merge_ss.at[i, 0], merge_rs.at[i, 0], seq=partner),
+            send(pair_st.at[i], merge_st.at[i], merge_ss.at[i, 1], merge_rs.at[i, 1], seq=partner),
+        )
+
+    def pass_on(slot, ss, where):
+        return send(att.at[slot], att.at[slot], ss, att_rs.at[slot], seq=where)
+
+    def ring(d):
+        return 2 * (y * 4 + (z + d) % 4) + c
+
+    def out_copy(g):
+        return send(rs_send.at[g], rs_recv.at[t], out_ss.at[g], out_rs.at[t], tp=g)
+
+    def out_arrival(i):
+        return send(rs_send.at[i], rs_recv.at[i], out_ss.at[i], out_rs.at[i], seq=partner)
+
+    def reach_of(j, parity):
+        return (1 + 3 * (j % 2)) * (1 + parity)
+
+    def in_order(i):
+        return (k // 2 * 2 + 2 * (i % 4) + i // 4) % chips
+
+    def start_pair(i, _):
+        j = in_order(i)
+
+        @pl.when(k < reach_of(j, 1 - c))
+        def _():
+            for copy in pair_copies(j):
+                copy.start()
+
+        return 0
+
+    lax.fori_loop(0, chips, start_pair, 0)
+
+    node = lax.broadcasted_iota(jnp.int32, (Q, Q), 0)
+    other = lax.broadcasted_iota(jnp.int32, (Q, Q), 1)
+    parent = jnp.broadcast_to(par_ref[pl.ds(s, 1), :], (Q, Q))
+    reach = jnp.where((node == other) | (node == parent), 1.0, 0.0)
     for _ in range((Q - 1).bit_length()):
-        reached = jnp.minimum(jnp.dot(reached, reached, preferred_element_type=jnp.float32), 1.0).astype(jnp.bfloat16)
-    return reached
-
-
-def local(queries, cache, draft_kv, out_weight, lengths, parents, path, accepted):
-    s = lax.axis_index("seq")
-    drafts = lax.all_gather(draft_kv, "seq", axis=1, tiled=True)
-    o, st, new_cache = attend(lengths, queries, cache)
-    m, l = st[:, 0, :], st[:, 1, :]
-    reach = closure(lax.dynamic_index_in_dim(parents, s, 0, False))
-    q = stacked_heads(lax.dynamic_slice_in_dim(queries, s * Q, Q, 0))
-    ds = lax.dot_general(draft_kv[0], q, (((1,), (1,)), ((), ())), preferred_element_type=jnp.float32)
-    ok = jnp.tile(reach.T, (1, q.shape[0] // Q)) > 0.5
-    ds = jnp.where(ok, ds, DEAD)
-    dm = jnp.max(ds, axis=0) * SCALE
-    dp = jnp.where(ok, jnp.exp2(ds * SCALE - dm), 0.0)
-    dl = jnp.sum(dp, axis=0)
-    do = lax.dot_general(draft_kv[1], dp.astype(jnp.bfloat16), (((0,), (0,)), ((), ())), preferred_element_type=jnp.float32)
-    mine = jnp.arange(m.shape[0]) == s
-    top = lax.pmax(jnp.maximum(m, jnp.where(mine[:, None], dm[None], DEAD)), "seq")
-    f = jnp.exp2(m - top)
-    df = jnp.where(mine[:, None], jnp.exp2(dm[None] - top), 0.0)
-    total = lax.psum(l * f + dl[None] * df, "seq")
-    part = (o.astype(jnp.float32) * f[:, None, :] + do[None] * df[:, None, :]) / total[:, None, :]
-    one = lax.psum_scatter(part, "seq", scatter_dimension=0, tiled=True)[0].astype(jnp.bfloat16)
-    heads = one.shape[1] // Q
-    one = one.reshape(HEAD, heads, Q).transpose(2, 1, 0).reshape(Q, heads * HEAD)
-    attended = lax.all_gather(one, "seq", axis=0, tiled=True)
-    attn_out = lax.psum_scatter(
-        jnp.dot(attended, out_weight, preferred_element_type=jnp.float32), "tp", scatter_dimension=0, tiled=True
-    ).astype(jnp.bfloat16)
-    return attn_out, commit(lengths, path, accepted, drafts, new_cache)
+        bits = reach.astype(jnp.bfloat16)
+        reach = jnp.minimum(jnp.dot(bits, bits, preferred_element_type=jnp.float32), 1.0)
+    lane = lax.broadcasted_iota(jnp.int32, (Q, width), 1) % Q
+    spread = jnp.where(lane == lax.broadcasted_iota(jnp.int32, (Q, width), 0), 1.0, 0.0).astype(jnp.bfloat16)
+    alive = jnp.dot(reach.astype(jnp.bfloat16), spread, preferred_element_type=jnp.float32) > 0.5
+    q_copy.wait()
+    scores = lax.dot_general(
+        dkv_ref[0], stacked_heads(q_ref[...]), (((1,), (1,)), ((), ())), preferred_element_type=jnp.float32
+    )
+    scores = jnp.where(alive, scores, DEAD)
+    peak = jnp.max(scores, axis=0, keepdims=True) * SCALE
+    weights = jnp.where(alive, jnp.exp2(scores * SCALE - peak), 0.0)
+    run_ref[0:1] = peak
+    run_ref[1:2] = jnp.sum(weights, axis=0, keepdims=True)
+    acc_ref[...] = jnp.dot(dkv_ref[1].T, weights.astype(jnp.bfloat16), preferred_element_type=jnp.float32)
+
+    def combine(i, _):
+        j = in_order(i)
+        r = 2 * j + c
+
+        @pl.when(k < reach_of(j, c))
+        def _():
+            for copy in pair_copies(j):
+                copy.wait_recv()
+            peak, total, a, b = folded_parts(
+                (st_ref[r, 0:1], st_ref[r, 1:2]), (pair_st[j, 0:1], pair_st[j, 1:2])
+            )
+            mixed = o_ref[r].astype(jnp.float32) * a + pair_o[j].astype(jnp.float32) * b
+            pair_o[j] = mixed.astype(jnp.bfloat16)
+            pair_st[j, 0:1] = peak
+            pair_st[j, 1:2] = total
+
+            @pl.when(j != k)
+            def _():
+                for copy in merge_copies(j):
+                    copy.start()
+
+        return 0
+
+    lax.fori_loop(0, chips, combine, 0)
+
+    def absorb(o, st):
+        peak, total, a, b = folded_parts((run_ref[0:1], run_ref[1:2]), (st[0:1], st[1:2]))
+        acc_ref[...] = acc_ref[...] * a + o[...].astype(jnp.float32) * b
+        run_ref[0:1] = peak
+        run_ref[1:2] = total
+
+    def merge(i, _):
+        j = (k + i) % chips
+
+        @pl.when(j < reach_of(k, c))
+        def _():
+            @pl.when(j == k)
+            def _():
+                absorb(pair_o.at[j], pair_st.at[j])
+
+            @pl.when(j != k)
+            def _():
+                for copy in merge_arrival(j):
+                    copy.wait_recv()
+                absorb(merge_o.at[j], merge_st.at[j])
+
+        return 0
+
+    lax.fori_loop(0, chips, merge, 0)
+
+    done = (acc_ref[...] / run_ref[1:2]).T.astype(jnp.bfloat16)
+    for h in range(heads):
+        att[s, :, h * HEAD : (h + 1) * HEAD] = done[h * Q : (h + 1) * Q]
+
+    twin = (k + 4) % chips
+    own = [pass_on(s, own_ss.at[0], 2 * twin + c)]
+    own += [pass_on(s, own_ss.at[d], ring(d)) for d in (1, 3, 2)]
+    own += [pass_on(s, own_ss.at[4], partner)]
+    for copy in own:
+        copy.start()
+
+    def group(i):
+        return (y + i // 2) % 2 * 4 + (z // 2 * 2 + 2 * i + i // 4) % 4
+
+    def forward(g):
+        return pass_on(2 * g + c, pass_ss.at[g], partner)
+
+    def relays():
+        return [pass_on(2 * twin + c, relay_ss.at[d], ring(d)) for d in (1, 3, 2)]
+
+    def arrival(slot):
+        return pass_on(slot, own_ss.at[0], partner)
+
+    def project(g):
+        arrival(2 * g + 1 - c).wait_recv()
+        rows = att[pl.ds(2 * g, 2)].reshape(2 * Q, att.shape[2])
+        rs_send[g] = jnp.dot(rows, w_ref[...], preferred_element_type=jnp.float32).astype(jnp.bfloat16)
+
+        @pl.when(g != t)
+        def _():
+            out_copy(g).start()
+
+    def spread_on(i, _):
+        g = group(i)
+
+        @pl.when(g != k)
+        def _():
+            arrival(2 * g + c).wait_recv()
+            forward(g).start()
+
+        @pl.when(g == twin)
+        def _():
+            for copy in relays():
+                copy.start()
+
+        @pl.when(i > 0)
+        def _():
+            project(group(i - 1))
+
+        return 0
+
+    lax.fori_loop(0, chips, spread_on, 0)
+    project(group(chips - 1))
+
+    total = rs_send[t].astype(jnp.float32)
+    for d in range(1, tps):
+        i = (t + d) % tps
+        out_arrival(i).wait_recv()
+        total = total + rs_recv[i].astype(jnp.float32)
+    out_ref[...] = total.astype(out_ref.dtype)
+
+    def finish_pair(j, _):
+        @pl.when(k < reach_of(j, 1 - c))
+        def _():
+            for copy in pair_copies(j):
+                copy.wait_send()
+
+        @pl.when((k < reach_of(j, c)) & (j != k))
+        def _():
+            for copy in merge_copies(j):
+                copy.wait_send()
+
+        @pl.when(j != k)
+        def _():
+            forward(j).wait_send()
+
+        @pl.when(j != t)
+        def _():
+            out_copy(j).wait_send()
+
+        return 0
+
+    lax.fori_loop(0, chips, finish_pair, 0)
+    for copy in own + relays():
+        copy.wait_send()
+
+
+def join(o, st, queries, draft_kv, parents, out_weight, chips, tps):
+    requests, _, width = o.shape
+    wide, columns = queries.shape[1], out_weight.shape[1]
+    dma = pltpu.SemaphoreType.DMA
+    whole = pl.BlockSpec(memory_space=pltpu.VMEM)
+    return pl.pallas_call(
+        join_kernel,
+        out_shape=jax.ShapeDtypeStruct((queries.shape[0] // tps, columns), jnp.bfloat16),
+        in_specs=[whole, whole, pl.BlockSpec(memory_space=pl.ANY), whole, whole, whole],
+        out_specs=whole,
+        scratch_shapes=[
+            pltpu.VMEM((Q, wide), jnp.bfloat16),
+            pltpu.VMEM((chips, HEAD, width), jnp.bfloat16),
+            pltpu.VMEM((chips, 8, width), jnp.float32),
+            pltpu.VMEM((chips, HEAD, width), jnp.bfloat16),
+            pltpu.VMEM((chips, 8, width), jnp.float32),
+            pltpu.VMEM((HEAD, width), jnp.float32),
+            pltpu.VMEM((8, width), jnp.float32),
+            pltpu.VMEM((requests, Q, wide), jnp.bfloat16),
+            pltpu.VMEM((tps, 2 * Q, columns), jnp.bfloat16),
+            pltpu.VMEM((tps, 2 * Q, columns), jnp.bfloat16),
+            dma,
+            dma((chips, 2)),
+            dma((chips, 2)),
+            dma((chips, 2)),
+            dma((chips, 2)),
+            dma((5,)),
+            dma((4,)),
+            dma((chips,)),
+            dma((requests,)),
+            dma((tps,)),
+            dma((tps,)),
+        ],
+        compiler_params=pltpu.CompilerParams(
+            collective_id=0, has_side_effects=True, vmem_limit_bytes=40 << 20
+        ),
+        name="join",
+    )(o, st, queries, draft_kv, parents, out_weight)
 
 
 def solution(mesh):
+    chips, tps = mesh.shape["seq"] // 2, mesh.shape["tp"]
+
+    def local(queries, cache, draft_kv, out_weight, lengths, parents, path, accepted):
+        drafts = lax.all_gather(draft_kv, "seq", axis=1, tiled=True)
+        o, st, new_cache = attend(lengths, queries, cache)
+        attn = join(o, st, queries, draft_kv, parents, out_weight, chips, tps)
+        return commit(lengths, path, accepted, drafts, attn, new_cache)
+
     return jax.shard_map(
         local,
         mesh=mesh,

time: 365 us -> 114 us (0.31); the launches traced: 359 us -> 113 us
  waiting for transfers between devices: 149 us -> 0 us
  blocking collectives: 148 us -> 21.2 us
  Pallas kernels: 16.1 us -> 86.1 us
  between operations: 13.9 us -> 0.73 us
  local copies, waits for them, and re-layouts: 16.5 us -> 4.7 us
  other arithmetic: 7.64 us -> 0 us
  matrix products: 7.63 us -> 0 us
    reduce_scatter x2 -> x0, waiting for transfers between devices: 101 us -> none  [the longest x1 84.4 us: local(): lax.psum_scatter(part, 'seq', scatter_dimension=0, tiled=True)[0]]
    psum x1 -> x0, blocking collectives: 65.5 us -> none  [local(): total = lax.psum(l * f + dl[None] * df, 'seq')]
    pallas_call x1 -> x2, Pallas kernels: 2.09 us -> 67.1 us  [the longest x1 64.3 us: join(): pl.pallas_call(join_kernel, out_shape=jax.ShapeDtypeStruct((queries.shape...]
    pmax x1 -> x0, blocking collectives: 61.4 us -> none  [local(): lax.pmax(jnp.maximum(m, jnp.where(mine[:, None], dm[None], DEAD)), 'seq')]
    all_gather x1 -> x0, waiting for transfers between devices: 48 us -> none  [local(): attended = lax.all_gather(one, 'seq', axis=0, tiled=True)]
    dot_general x6 -> x0, matrix products: 7.63 us -> none  [the longest x1 4.18 us: local(): jnp.dot(attended, out_weight, preferred_element_type=jnp.float32)]
    unnamed x20 -> x15, local copies, waits for them, and re-layouts: 12 us -> 4.7 us
    pallas_call x1, Pallas kernels: 14.1 us -> 19.1 us  [attend(): pl.pallas_call(attend_kernel, out_shape=(jax.ShapeDtypeStruct((requests,...]
  transfers between devices with their start and end apart: 3 -> 0, of which waited for: 3 -> 0; matrix products, arithmetic and copies ran while one was open for 0% -> 0% of each run, Pallas kernels for 1% -> 0%
where the time goes in v2:
time: 114 us; the launch traced here: 113 us
  Pallas kernels  86.1 us (76%)
  blocking collectives  21.2 us (19%)
  local copies, waits for them, and re-layouts  4.7 us (4%)
    pallas_call x1, Pallas kernels, join(): pl.pallas_call(join_kernel, out_shape=jax.ShapeDtypeStruct((queries.shape...  64.3 us
    all_gather x1, blocking collectives, local(): drafts = lax.all_gather(draft_kv, 'seq', axis=1, tiled=True)  21.2 us
    pallas_call x1, Pallas kernels, attend(): pl.pallas_call(attend_kernel, out_shape=(jax.ShapeDtypeStruct((requests,...  19.1 us
    unnamed x15, local copies, waits for them, and re-layouts  4.7 us
    pallas_call x1, Pallas kernels, commit(): pl.pallas_call(commit_kernel, out_shape=(jax.ShapeDtypeStruct(attn.shape,...  2.76 us

profile of v2, /device:TPU:114, one launch (start us, length us, event | category | flops | bytes accessed | tf_op | source)
XLA Modules:
  0.0 112.7 jit_solution(7934288914502241495)
XLA Ops:
  0.6 0.0 copy-start.5
  0.6 0.0 copy-start
  0.7 0.0 copy-start.6
  0.7 0.0 copy-start.2
  0.7 1.5 %copy.11.path_ref = s32[16,8]{1,0:T(8,128)} copy(s32[16,8]{0,1:T(8,128)} %param.14) | data formatting | bytes 1024 | tf_op args[6]
  2.2 21.2 %all_gather.3.draft_ref = bf16[2,1024,128]{2,1,0:T(8,128)(2,1)} all-gather(bf16[2,64,128]{2,1,0:T(8,128)(2,1)} %dkv_ref.1), channel_id=1, replica_groups=mesh['seq'=16,'tp'=8] {'seq'}, dimensions={1}, use_global_device_ids=true | all-gather | bytes 557056 | tf_op jit(solution)/shard_map/all_gather | solution.py:517
  23.4 19.1 %attend.1 = (bf16[16,128,512]{2,1,0:T(8,128)(2,1)}, f32[16,8,512]{2,1,0:T(8,128)}, bf16[2,16,1024,128]{3,2,1,0:T(8,128)(2,1)}) custom-call(s32[16]{0:T(128)} %len_ref.3, bf16[1024,1024]{1,0:T(8,128)(2,1)} %q_hbm.1, bf16[2,16,1024,128]{3,2,1,0:T(8,128)(2,1)} %kv_ref.1), custom_call_target="tpu_custom_call" | custom-call | tf_op jit(solution)/shard_map/attend/pallas_call | solution.py:108
  42.4 0.0 copy-done.5
  42.5 0.0 copy-done
  42.5 0.0 copy-done.6
  42.5 0.0 copy-done.2
  42.5 0.0 copy-start.1
  42.5 1.6 %copy-done.1 = bf16[16,128,512]{2,1,0:T(8,128)(2,1)S(1)} copy-done((bf16[16,128,512]{2,1,0:T(8,128)(2,1)S(1)}, bf16[16,128,512]{2,1,0:T(8,128)(2,1)}, u32[]{:S(2)}) %copy-start.1) | copy-done | bytes 2097176
  44.1 0.0 copy-start.4
  44.1 0.9 copy-done.4
  45.0 64.3 %join.1.attn_ref = bf16[128,512]{1,0:T(8,128)(2,1)S(1)} custom-call(bf16[16,128,512]{2,1,0:T(8,128)(2,1)S(1)} %copy-done.1, f32[16,8,512]{2,1,0:T(8,128)S(1)} %copy-done.4, bf16[1024,1024]{1,0:T(8,128)(2,1)S(1)} %copy-done, bf16[2,64,128]{2,1,0:T(8,128)(2,1)S(1)} %copy-done.5, s32[16,64]{1,0:T(8,128)S(1)} %copy-done.6, bf16[1024,512]{1,0:T(8,128)(2,1)S(1)} %copy-done.2), custom_call_target="tpu_custom_call" | custom-call | tf_op jit(solution)/shard_map/join/pallas_call | solution.py:478
  109.3 0.0 copy-start.3
  109.3 0.6 copy-done.3
  110.0 2.8 %commit.1 = (bf16[128,512]{1,0:T(8,128)(2,1)}, bf16[2,16,1024,128]{3,2,1,0:T(8,128)(2,1)}) custom-call(s32[16]{0:T(128)} %len_ref.3, s32[16,8]{1,0:T(8,128)} %copy.11.path_ref, s32[16]{0:T(128)} %acc_ref.1, bf16[2,1024,128]{2,1,0:T(8,128)(2,1)} %all_gather.3.draft_ref, bf16[128,512]{1,0:T(8,128)(2,1)} %copy-done.3, ...), custom_call_target="tpu_custom_call", output_to_operand_aliasing={{1}: (5, {})} | custom-call | tf_op jit(solution)/shard_map/commit/pallas_call | solution.py:212
Async XLA Ops:
  0.6 41.8 %copy-start.5 = (bf16[2,64,128]{2,1,0:T(8,128)(2,1)S(1)}, bf16[2,64,128]{2,1,0:T(8,128)(2,1)}, u32[]{:S(2)}) copy-start(bf16[2,64,128]{2,1,0:T(8,128)(2,1)} %dkv_ref.1) | copy-start | bytes 98308
  0.6 41.8 %copy-start = (bf16[1024,1024]{1,0:T(8,128)(2,1)S(1)}, bf16[1024,1024]{1,0:T(8,128)(2,1)}, u32[]{:S(2)}) copy-start(bf16[1024,1024]{1,0:T(8,128)(2,1)} %q_hbm.1) | copy-start | bytes 6291460
  0.7 41.8 %copy-start.6 = (s32[16,64]{1,0:T(8,128)S(1)}, s32[16,64]{1,0:T(8,128)}, u32[]{:S(2)}) copy-start(s32[16,64]{1,0:T(8,128)} %par_ref.1) | copy-start | bytes 12292
  0.7 41.8 %copy-start.2 = (bf16[1024,512]{1,0:T(8,128)(2,1)S(1)}, bf16[1024,512]{1,0:T(8,128)(2,1)}, u32[]{:S(2)}) copy-start(bf16[1024,512]{1,0:T(8,128)(2,1)} %w_ref.1) | copy-start | bytes 3145732
  42.5 1.6 %copy-start.1 = (bf16[16,128,512]{2,1,0:T(8,128)(2,1)S(1)}, bf16[16,128,512]{2,1,0:T(8,128)(2,1)}, u32[]{:S(2)}) copy-start(bf16[16,128,512]{2,1,0:T(8,128)(2,1)} %get-tuple-element.5.o_ref) | copy-start | bytes 6291460
  44.1 0.9 copy-start.4
  109.3 0.7 copy-start.3

commit v3 on v2

--- a/solution.py
+++ b/solution.py
@@ -22,89 +22,120 @@
     return jnp.concatenate([rows[:, h * HEAD : (h + 1) * HEAD] for h in range(heads)], axis=0)
 
 
-def attend_kernel(len_ref, q_ref, kv_ref, o_ref, st_ref, nc_ref, s_ref, acc_ref, max_ref, sem):
-    span = kv_ref.shape[2]
+def attend_kernel(
+    len_ref, q_hbm, kv_hbm, o_ref, st_ref, nc_ref, q_ref, kv_ref, s_ref, acc_ref, max_ref, q_sem, load_sem, store_sem
+):
+    requests, span = kv_ref.shape[0], kv_ref.shape[2]
     chunks = span // CHUNK
     width = s_ref.shape[1]
-    r = pl.program_id(0)
-    live = jnp.clip(len_ref[r] - lax.axis_index("seq") * span, 0, span)
-    copy = pltpu.make_async_copy(kv_ref, nc_ref.at[:, pl.ds(r, 1)], sem)
-    copy.start()
-
-    def scores(at):
-        return lax.dot_general(
-            kv_ref[0, 0, pl.ds(at, CHUNK), :],
-            stacked_heads(q_ref[...]),
-            (((1,), (1,)), ((), ())),
-            preferred_element_type=jnp.float32,
-        )
-
-    def folded(s):
-        return jnp.max(s.reshape(CHUNK // 8, 8, width), axis=0)
-
-    def weighted(at, p):
-        values = kv_ref[1, 0, pl.ds(at, CHUNK), :].T
-        values = jnp.concatenate([values, jnp.ones((16, CHUNK), values.dtype)], axis=0)
-        return jnp.dot(values, p, preferred_element_type=jnp.float32)
-
-    def publish(peak, acc):
-        o_ref[0] = acc[:HEAD].astype(o_ref.dtype)
-        st_ref[0, 0:1] = peak
-        st_ref[0, 1:2] = acc[HEAD : HEAD + 1]
-
-    @pl.when(live == 0)
-    def _():
-        publish(jnp.full((1, width), DEAD, jnp.float32), jnp.zeros((HEAD + 16, width), jnp.float32))
-
-    @pl.when(live == span)
-    def _():
-        peak = None
-        for c in range(chunks):
-            s = scores(c * CHUNK)
-            s_ref[pl.ds(c * CHUNK, CHUNK), :] = s
-            peak = folded(s) if peak is None else jnp.maximum(peak, folded(s))
-        peak = jnp.max(peak, axis=0, keepdims=True) * SCALE
-        acc = None
-        for c in range(chunks):
-            p = jnp.exp2(s_ref[pl.ds(c * CHUNK, CHUNK), :] * SCALE - peak).astype(jnp.bfloat16)
-            term = weighted(c * CHUNK, p)
-            acc = term if acc is None else acc + term
-        publish(peak, acc)
-
-    @pl.when((live > 0) & (live < span))
-    def _():
-        used = (live + CHUNK - 1) // CHUNK
-        max_ref[...] = jnp.full_like(max_ref, DEAD)
-        acc_ref[...] = jnp.zeros_like(acc_ref)
-
-        def first(c, _):
-            at = pl.multiple_of(c * CHUNK, CHUNK)
-            row = lax.broadcasted_iota(jnp.int32, (CHUNK, width), 0) + at
-            s = jnp.where(row < live, scores(at), DEAD)
-            s_ref[pl.ds(at, CHUNK), :] = s
-            max_ref[...] = jnp.maximum(max_ref[...], folded(s))
-            return 0
-
-        lax.fori_loop(0, used, first, 0)
-        peak = jnp.max(max_ref[...], axis=0, keepdims=True) * SCALE
-
-        def second(c, _):
-            at = pl.multiple_of(c * CHUNK, CHUNK)
-            row = lax.broadcasted_iota(jnp.int32, (CHUNK, width), 0) + at
-            p = jnp.exp2(s_ref[pl.ds(at, CHUNK), :] * SCALE - peak)
-            p = jnp.where(row < live, p, 0.0).astype(jnp.bfloat16)
-            acc_ref[...] += weighted(at, p)
-            return 0
-
-        lax.fori_loop(0, used, second, 0)
-        publish(peak, acc_ref[...])
-
-    copy.wait()
+    base = lax.axis_index("seq") * span
+
+    def q_load(r):
+        rows = pl.ds(pl.multiple_of(r * Q, Q), Q)
+        return pltpu.make_async_copy(q_hbm.at[rows, :], q_ref.at[r], q_sem.at[r])
+
+    def load(r):
+        return pltpu.make_async_copy(kv_hbm.at[:, r], kv_ref.at[r], load_sem.at[r])
+
+    def store(r):
+        return pltpu.make_async_copy(kv_ref.at[r], nc_ref.at[:, r], store_sem.at[r])
+
+    def begin(r, _):
+        q_load(r).start()
+        load(r).start()
+        return 0
+
+    lax.fori_loop(0, requests, begin, 0)
+
+    def one(r, _):
+        live = jnp.clip(len_ref[r] - base, 0, span)
+        q_load(r).wait()
+        load(r).wait()
+        store(r).start()
+
+        def scores(at):
+            return lax.dot_general(
+                kv_ref[r, 0, pl.ds(at, CHUNK), :],
+                stacked_heads(q_ref[r]),
+                (((1,), (1,)), ((), ())),
+                preferred_element_type=jnp.float32,
+            )
+
+        def folded(s):
+            return jnp.max(s.reshape(CHUNK // 8, 8, width), axis=0)
+
+        def weighted(at, p):
+            values = kv_ref[r, 1, pl.ds(at, CHUNK), :].T
+            values = jnp.concatenate([values, jnp.ones((16, CHUNK), values.dtype)], axis=0)
+            return jnp.dot(values, p, preferred_element_type=jnp.float32)
+
+        def publish(peak, acc):
+            o_ref[r] = acc[:HEAD].astype(o_ref.dtype)
+            st_ref[r, 0:1] = peak
+            st_ref[r, 1:2] = acc[HEAD : HEAD + 1]
+
+        @pl.when(live == 0)
+        def _():
+            publish(jnp.full((1, width), DEAD, jnp.float32), jnp.zeros((HEAD + 16, width), jnp.float32))
+
+        @pl.when(live == span)
+        def _():
+            peak = None
+            for c in range(chunks):
+                s = scores(c * CHUNK)
+                s_ref[pl.ds(c * CHUNK, CHUNK), :] = s
+                peak = folded(s) if peak is None else jnp.maximum(peak, folded(s))
+            peak = jnp.max(peak, axis=0, keepdims=True) * SCALE
+            acc = None
+            for c in range(chunks):
+                p = jnp.exp2(s_ref[pl.ds(c * CHUNK, CHUNK), :] * SCALE - peak).astype(jnp.bfloat16)
+                term = weighted(c * CHUNK, p)
+                acc = term if acc is None else acc + term
+            publish(peak, acc)
+
+        @pl.when((live > 0) & (live < span))
+        def _():
+            used = (live + CHUNK - 1) // CHUNK
+            max_ref[...] = jnp.full_like(max_ref, DEAD)
+            acc_ref[...] = jnp.zeros_like(acc_ref)
+
+            def first(c, _):
+                at = pl.multiple_of(c * CHUNK, CHUNK)
+                row = lax.broadcasted_iota(jnp.int32, (CHUNK, width), 0) + at
+                s = jnp.where(row < live, scores(at), DEAD)
+                s_ref[pl.ds(at, CHUNK), :] = s
+                max_ref[...] = jnp.maximum(max_ref[...], folded(s))
+                return 0
+
+            lax.fori_loop(0, used, first, 0)
+            peak = jnp.max(max_ref[...], axis=0, keepdims=True) * SCALE
+
+            def second(c, _):
+                at = pl.multiple_of(c * CHUNK, CHUNK)
+                row = lax.broadcasted_iota(jnp.int32, (CHUNK, width), 0) + at
+                p = jnp.exp2(s_ref[pl.ds(at, CHUNK), :] * SCALE - peak)
+                p = jnp.where(row < live, p, 0.0).astype(jnp.bfloat16)
+                acc_ref[...] += weighted(at, p)
+                return 0
+
+            lax.fori_loop(0, used, second, 0)
+            publish(peak, acc_ref[...])
+
+        return 0
+
+    lax.fori_loop(0, requests, one, 0)
+
+    def end(r, _):
+        store(r).wait()
+        return 0
+
+    lax.fori_loop(0, requests, end, 0)
 
 
 def attend(lengths, queries, cache):
     requests, span = cache.shape[1], cache.shape[2]
-    width = queries.shape[1] // HEAD * Q
+    wide = queries.shape[1]
+    width = wide // HEAD * Q
     return pl.pallas_call(
         attend_kernel,
         out_shape=(
@@ -112,32 +143,33 @@
             jax.ShapeDtypeStruct((requests, 8, width), jnp.float32),
             jax.ShapeDtypeStruct(cache.shape, cache.dtype),
         ),
-        grid_spec=pltpu.PrefetchScalarGridSpec(
-            num_scalar_prefetch=1,
-            grid=(requests,),
-            in_specs=[
-                pl.BlockSpec((Q, queries.shape[1]), lambda r, n: (r, 0)),
-                pl.BlockSpec((2, 1, span, HEAD), lambda r, n: (0, r, 0, 0)),
-            ],
-            out_specs=(
-                pl.BlockSpec((1, HEAD, width), lambda r, n: (r, 0, 0)),
-                pl.BlockSpec((1, 8, width), lambda r, n: (r, 0, 0)),
-                pl.BlockSpec(memory_space=pl.ANY),
-            ),
-            scratch_shapes=[
-                pltpu.VMEM((span, width), jnp.float32),
-                pltpu.VMEM((HEAD + 16, width), jnp.float32),
-                pltpu.VMEM((8, width), jnp.float32),
-                pltpu.SemaphoreType.DMA,
-            ],
+        in_specs=[
+            pl.BlockSpec(memory_space=pltpu.SMEM),
+            pl.BlockSpec(memory_space=pltpu.HBM),
+            pl.BlockSpec(memory_space=pltpu.HBM),
+        ],
+        out_specs=(
+            pl.BlockSpec(memory_space=pltpu.VMEM),
+            pl.BlockSpec(memory_space=pltpu.VMEM),
+            pl.BlockSpec(memory_space=pltpu.HBM),
         ),
-        compiler_params=pltpu.CompilerParams(vmem_limit_bytes=56 << 20),
+        scratch_shapes=[
+            pltpu.VMEM((requests, Q, wide), jnp.bfloat16),
+            pltpu.VMEM((requests, 2, span, HEAD), jnp.bfloat16),
+            pltpu.VMEM((span, width), jnp.float32),
+            pltpu.VMEM((HEAD + 16, width), jnp.float32),
+            pltpu.VMEM((8, width), jnp.float32),
+            pltpu.SemaphoreType.DMA((requests,)),
+            pltpu.SemaphoreType.DMA((requests,)),
+            pltpu.SemaphoreType.DMA((requests,)),
+        ],
+        compiler_params=pltpu.CompilerParams(vmem_limit_bytes=60 << 20),
         name="attend",
     )(lengths, queries, cache)
 
 
 def commit_kernel(
-    len_ref, path_ref, acc_ref, draft_ref, attn_ref, nc_in, out_ref, nc_ref, win_ref, load_sem, store_sem
+    len_ref, acc_ref, chosen_ref, attn_ref, nc_in, out_ref, nc_ref, win_ref, load_sem, store_sem
 ):
     requests, span = nc_ref.shape[1], nc_ref.shape[2]
     base = lax.axis_index("seq") * span
@@ -172,18 +204,16 @@
 
         @pl.when(hit)
         def _():
-            row = lax.broadcasted_iota(jnp.int32, (WINDOW, Q), 0) + (start - off)
-            node = lax.broadcasted_iota(jnp.int32, (WINDOW, Q), 1)
-            pick = jnp.zeros((WINDOW, Q), jnp.float32)
-            for j in range(ACC):
-                pick = jnp.where((row == j) & (node == path_ref[r, j]), 1.0, pick)
+            row = lax.broadcasted_iota(jnp.int32, (WINDOW, 2 * ACC), 0) + (start - off)
+            node = lax.broadcasted_iota(jnp.int32, (WINDOW, 2 * ACC), 1)
+            pick = jnp.where(row == node, 1.0, 0.0).astype(jnp.bfloat16)
             slot = lax.broadcasted_iota(jnp.int32, (WINDOW, HEAD), 0) + (start - off)
             fresh = (slot >= 0) & (slot < acc_ref[r])
             load(r, start).wait()
             for x in range(2):
                 rows = jnp.dot(
-                    pick.astype(jnp.bfloat16),
-                    draft_ref[x, pl.ds(pl.multiple_of(r * Q, Q), Q), :],
+                    pick,
+                    chosen_ref[r, 2 * ACC * x : 2 * ACC * (x + 1)],
                     preferred_element_type=jnp.float32,
                 )
                 old = win_ref[r, x].astype(jnp.float32)
@@ -207,7 +237,7 @@
     lax.fori_loop(0, requests, end, 0)
 
 
-def commit(lengths, path, accepted, drafts, attn, new_cache):
+def commit(lengths, accepted, chosen, attn, new_cache):
     requests = new_cache.shape[1]
     return pl.pallas_call(
         commit_kernel,
@@ -215,7 +245,7 @@
             jax.ShapeDtypeStruct(attn.shape, attn.dtype),
             jax.ShapeDtypeStruct(new_cache.shape, new_cache.dtype),
         ),
-        in_specs=[pl.BlockSpec(memory_space=pltpu.SMEM)] * 3
+        in_specs=[pl.BlockSpec(memory_space=pltpu.SMEM)] * 2
         + [pl.BlockSpec(memory_space=pltpu.VMEM)] * 2
         + [pl.BlockSpec(memory_space=pl.ANY)],
         out_specs=(pl.BlockSpec(memory_space=pltpu.VMEM), pl.BlockSpec(memory_space=pl.ANY)),
@@ -224,9 +254,9 @@
             pltpu.SemaphoreType.DMA((requests,)),
             pltpu.SemaphoreType.DMA((requests,)),
         ],
-        input_output_aliases={5: 1},
+        input_output_aliases={4: 1},
         name="commit",
-    )(lengths, path, accepted, drafts, attn, new_cache)
+    )(lengths, accepted, chosen, attn, new_cache)
 
 
 def folded_parts(first, second):
@@ -236,9 +266,9 @@
 
 
 def join_kernel(
-    o_ref, st_ref, q_hbm, dkv_ref, par_ref, w_ref, out_ref,
-    q_ref, pair_o, pair_st, merge_o, merge_st, acc_ref, run_ref, att, rs_send, rs_recv,
-    q_sem, pair_ss, pair_rs, merge_ss, merge_rs, own_ss, relay_ss, pass_ss, att_rs, out_ss, out_rs,
+    o_hbm, st_hbm, q_hbm, dkv_ref, par_ref, path_ref, w_hbm, out_ref, chosen_ref,
+    q_ref, o_ref, st_ref, w_ref, pair_o, pair_st, merge_o, merge_st, acc_ref, run_ref, att, rs_send, rs_recv,
+    q_sem, in_sem, pair_ss, pair_rs, merge_ss, merge_rs, own_ss, relay_ss, pass_ss, att_rs, out_ss, out_rs,
 ):
     s, t = lax.axis_index("seq"), lax.axis_index("tp")
     k, c = s // 2, s % 2
@@ -256,6 +286,13 @@
         pl.semaphore_signal(barrier, inc=1, device_id={"tp": (t + d) % tps}, device_id_type=MESH)
     q_copy = pltpu.make_async_copy(q_hbm.at[pl.ds(pl.multiple_of(s * Q, Q), Q), :], q_ref, q_sem)
     q_copy.start()
+    w_copy = pltpu.make_async_copy(w_hbm, w_ref, in_sem.at[0])
+    o_copy = pltpu.make_async_copy(o_hbm, o_ref, in_sem.at[1])
+    st_copy = pltpu.make_async_copy(st_hbm, st_ref, in_sem.at[2])
+    for copy in (o_copy, st_copy, w_copy):
+        copy.start()
+    o_copy.wait()
+    st_copy.wait()
     pl.semaphore_wait(barrier, chips + tps - 1)
 
     def send(src, dst, ss, rs, **where):
@@ -383,9 +420,14 @@
 
     lax.fori_loop(0, chips, merge, 0)
 
-    done = (acc_ref[...] / run_ref[1:2]).T.astype(jnp.bfloat16)
-    for h in range(heads):
-        att[s, :, h * HEAD : (h + 1) * HEAD] = done[h * Q : (h + 1) * Q]
+    att[s, :width] = (acc_ref[...] / run_ref[1:2]).T.astype(jnp.bfloat16)
+    lanes = lax.broadcasted_iota(jnp.int32, path_ref.shape, 1)
+    nodes = jnp.sum(jnp.where(lanes == s, path_ref[...], 0), axis=1, keepdims=True)
+    pick = jnp.where(lax.broadcasted_iota(jnp.int32, (ACC, Q), 1) == nodes, 1.0, 0.0)
+    pick = jnp.concatenate([pick, jnp.zeros((ACC, Q), jnp.float32)], axis=0).astype(jnp.bfloat16)
+    for x in range(2):
+        rows = jnp.dot(pick, dkv_ref[x], preferred_element_type=jnp.float32)
+        att[s, width + 2 * ACC * x : width + 2 * ACC * (x + 1)] = rows.astype(jnp.bfloat16)
 
     twin = (k + 4) % chips
     own = [pass_on(s, own_ss.at[0], 2 * twin + c)]
@@ -408,7 +450,13 @@
 
     def project(g):
         arrival(2 * g + 1 - c).wait_recv()
-        rows = att[pl.ds(2 * g, 2)].reshape(2 * Q, att.shape[2])
+        rows = jnp.concatenate(
+            [
+                jnp.concatenate([att[2 * g, h * Q : (h + 1) * Q], att[2 * g + 1, h * Q : (h + 1) * Q]], axis=0)
+                for h in range(heads)
+            ],
+            axis=1,
+        )
         rs_send[g] = jnp.dot(rows, w_ref[...], preferred_element_type=jnp.float32).astype(jnp.bfloat16)
 
         @pl.when(g != t)
@@ -434,6 +482,7 @@
 
         return 0
 
+    w_copy.wait()
     lax.fori_loop(0, chips, spread_on, 0)
     project(group(chips - 1))
 
@@ -443,6 +492,7 @@
         out_arrival(i).wait_recv()
         total = total + rs_recv[i].astype(jnp.float32)
     out_ref[...] = total.astype(out_ref.dtype)
+    chosen_ref[...] = att[:, width:]
 
     def finish_pair(j, _):
         @pl.when(k < reach_of(j, 1 - c))
@@ -470,28 +520,35 @@
         copy.wait_send()
 
 
-def join(o, st, queries, draft_kv, parents, out_weight, chips, tps):
+def join(o, st, queries, draft_kv, parents, path, out_weight, chips, tps):
     requests, _, width = o.shape
     wide, columns = queries.shape[1], out_weight.shape[1]
     dma = pltpu.SemaphoreType.DMA
-    whole = pl.BlockSpec(memory_space=pltpu.VMEM)
+    whole, far = pl.BlockSpec(memory_space=pltpu.VMEM), pl.BlockSpec(memory_space=pl.ANY)
     return pl.pallas_call(
         join_kernel,
-        out_shape=jax.ShapeDtypeStruct((queries.shape[0] // tps, columns), jnp.bfloat16),
-        in_specs=[whole, whole, pl.BlockSpec(memory_space=pl.ANY), whole, whole, whole],
-        out_specs=whole,
+        out_shape=(
+            jax.ShapeDtypeStruct((queries.shape[0] // tps, columns), jnp.bfloat16),
+            jax.ShapeDtypeStruct((requests, 4 * ACC, HEAD), jnp.bfloat16),
+        ),
+        in_specs=[far, far, far, whole, whole, whole, far],
+        out_specs=(whole, whole),
         scratch_shapes=[
             pltpu.VMEM((Q, wide), jnp.bfloat16),
+            pltpu.VMEM(o.shape, o.dtype),
+            pltpu.VMEM(st.shape, st.dtype),
+            pltpu.VMEM(out_weight.shape, out_weight.dtype),
             pltpu.VMEM((chips, HEAD, width), jnp.bfloat16),
             pltpu.VMEM((chips, 8, width), jnp.float32),
             pltpu.VMEM((chips, HEAD, width), jnp.bfloat16),
             pltpu.VMEM((chips, 8, width), jnp.float32),
             pltpu.VMEM((HEAD, width), jnp.float32),
             pltpu.VMEM((8, width), jnp.float32),
-            pltpu.VMEM((requests, Q, wide), jnp.bfloat16),
+            pltpu.VMEM((requests, width + 4 * ACC, HEAD), jnp.bfloat16),
             pltpu.VMEM((tps, 2 * Q, columns), jnp.bfloat16),
             pltpu.VMEM((tps, 2 * Q, columns), jnp.bfloat16),
             dma,
+            dma((3,)),
             dma((chips, 2)),
             dma((chips, 2)),
             dma((chips, 2)),
@@ -504,20 +561,19 @@
             dma((tps,)),
         ],
         compiler_params=pltpu.CompilerParams(
-            collective_id=0, has_side_effects=True, vmem_limit_bytes=40 << 20
+            collective_id=0, has_side_effects=True, vmem_limit_bytes=60 << 20
         ),
         name="join",
-    )(o, st, queries, draft_kv, parents, out_weight)
+    )(o, st, queries, draft_kv, parents, path, out_weight)
 
 
 def solution(mesh):
     chips, tps = mesh.shape["seq"] // 2, mesh.shape["tp"]
 
     def local(queries, cache, draft_kv, out_weight, lengths, parents, path, accepted):
-        drafts = lax.all_gather(draft_kv, "seq", axis=1, tiled=True)
         o, st, new_cache = attend(lengths, queries, cache)
-        attn = join(o, st, queries, draft_kv, parents, out_weight, chips, tps)
-        return commit(lengths, path, accepted, drafts, attn, new_cache)
+        attn, chosen = join(o, st, queries, draft_kv, parents, path.T, out_weight, chips, tps)
+        return commit(lengths, accepted, chosen, attn, new_cache)
 
     return jax.shard_map(
         local,

time: 114 us -> 82.6 us (0.72)
  blocking collectives: 21.2 us -> 0 us
  local copies, waits for them, and re-layouts: 4.7 us -> 0 us
  Pallas kernels: 86.1 us -> 81.8 us
    all_gather x1 -> x0, blocking collectives: 21.2 us -> none  [local(): drafts = lax.all_gather(draft_kv, 'seq', axis=1, tiled=True)]
    pallas_call x1, Pallas kernels: 19.1 us -> 9.94 us  [attend(): pl.pallas_call(attend_kernel, out_shape=(jax.ShapeDtypeStruct((requests,...]
    unnamed x15 -> x0, local copies, waits for them, and re-layouts: 4.7 us -> none
    pallas_call x1, Pallas kernels: 64.3 us -> 68.2 us  [join(): pl.pallas_call(join_kernel, out_shape=(jax.ShapeDtypeStruct((queries.shap...]
where the time goes in v3:
time: 82.6 us; the launch traced here: 82.4 us
  Pallas kernels  81.8 us (99%)
    pallas_call x1, Pallas kernels, join(): pl.pallas_call(join_kernel, out_shape=(jax.ShapeDtypeStruct((queries.shap...  68.2 us
    pallas_call x1, Pallas kernels, attend(): pl.pallas_call(attend_kernel, out_shape=(jax.ShapeDtypeStruct((requests,...  9.94 us
    pallas_call x1, Pallas kernels, commit(): pl.pallas_call(commit_kernel, out_shape=(jax.ShapeDtypeStruct(attn.shape,...  3.62 us

profile of v3, /device:TPU:114, one launch (start us, length us, event | category | flops | bytes accessed | tf_op | source)
XLA Modules:
  0.0 82.4 jit_solution(10193760712328417122)
XLA Ops:
  0.6 9.9 %attend.1 = (bf16[16,128,512]{2,1,0:T(8,128)(2,1)}, f32[16,8,512]{2,1,0:T(8,128)}, bf16[2,16,1024,128]{3,2,1,0:T(8,128)(2,1)}) custom-call(s32[16]{0:T(128)} %len_ref.3, bf16[1024,1024]{1,0:T(8,128)(2,1)} %q_hbm.3, bf16[2,16,1024,128]{3,2,1,0:T(8,128)(2,1)} %kv_hbm.1), custom_call_target="tpu_custom_call" | custom-call | tf_op jit(solution)/shard_map/attend/pallas_call | solution.py:139
  10.6 68.2 %join.1 = (bf16[128,512]{1,0:T(8,128)(2,1)}, bf16[16,32,128]{2,1,0:T(8,128)(2,1)}) custom-call(bf16[16,128,512]{2,1,0:T(8,128)(2,1)} %get-tuple-element.7.o_hbm, f32[16,8,512]{2,1,0:T(8,128)} %get-tuple-element.8.st_hbm, bf16[1024,1024]{1,0:T(8,128)(2,1)} %q_hbm.3, bf16[2,64,128]{2,1,0:T(8,128)(2,1)} %dkv_ref.1, s32[16,64]{1,0:T(8,128)} %par_ref.1, ...), custom_call_target="tpu_custom_call" | custom-call | tf_op jit(solution)/shard_map/join/pallas_call | solution.py:528
  78.8 3.6 %commit.1 = (bf16[128,512]{1,0:T(8,128)(2,1)}, bf16[2,16,1024,128]{3,2,1,0:T(8,128)(2,1)}) custom-call(s32[16]{0:T(128)} %len_ref.3, s32[16]{0:T(128)} %acc_ref.1, bf16[16,32,128]{2,1,0:T(8,128)(2,1)} %get-tuple-element.9.chosen_ref, bf16[128,512]{1,0:T(8,128)(2,1)} %get-tuple-element.10.attn_ref, ...), custom_call_target="tpu_custom_call", output_to_operand_aliasing={{1}: (4, {})} | custom-call | tf_op jit(solution)/shard_map/commit/pallas_call | solution.py:242

commit v4 on v3

--- a/solution.py
+++ b/solution.py
@@ -22,146 +22,175 @@
     return jnp.concatenate([rows[:, h * HEAD : (h + 1) * HEAD] for h in range(heads)], axis=0)
 
 
+def score_chunk(kv, q, c, live):
+    s = lax.dot_general(
+        kv[0, c * CHUNK : (c + 1) * CHUNK, :], q, (((1,), (1,)), ((), ())), preferred_element_type=jnp.float32
+    )
+    row = lax.broadcasted_iota(jnp.int32, s.shape, 0) + c * CHUNK
+    return jnp.where(row < live, s, DEAD)
+
+
+def attention_step(now, s_now, peak_now, later, q_later, live, s_later):
+    acc = peak = None
+    for c in range(s_now.shape[0] // CHUNK):
+        rows = slice(c * CHUNK, (c + 1) * CHUNK)
+        if later is not None:
+            s = score_chunk(later, q_later, c, live)
+            s_later[rows, :] = s
+            top = jnp.max(s.reshape(CHUNK // 8, 8, s.shape[1]), axis=0)
+            peak = top if peak is None else jnp.maximum(peak, top)
+        if now is not None:
+            p = jnp.exp2(s_now[rows, :] * SCALE - peak_now).astype(jnp.bfloat16)
+            values = now[1, rows, :].T
+            values = jnp.concatenate([values, jnp.ones((16, CHUNK), values.dtype)], axis=0)
+            term = jnp.dot(values, p, preferred_element_type=jnp.float32)
+            acc = term if acc is None else acc + term
+    if peak is not None:
+        peak = jnp.max(peak, axis=0, keepdims=True) * SCALE
+    return acc, peak
+
+
+def publish(o, st, peak, acc):
+    o[...] = acc[:HEAD].astype(o.dtype)
+    st[0:1] = peak
+    st[1:2] = acc[HEAD : HEAD + 1]
+
+
 def attend_kernel(
-    len_ref, q_hbm, kv_hbm, o_ref, st_ref, nc_ref, q_ref, kv_ref, s_ref, acc_ref, max_ref, q_sem, load_sem, store_sem
+    len_ref, q_hbm, kv_hbm, o_hbm, st_hbm, nc_hbm,
+    q_ref, kv_ref, o_ref, st_ref, s_ref, peak_ref, job_ref, q_sem, load_sem, store_sem, out_sem,
 ):
     requests, span = kv_ref.shape[0], kv_ref.shape[2]
-    chunks = span // CHUNK
-    width = s_ref.shape[1]
+    few = o_ref.shape[0]
     base = lax.axis_index("seq") * span
 
-    def q_load(r):
-        rows = pl.ds(pl.multiple_of(r * Q, Q), Q)
-        return pltpu.make_async_copy(q_hbm.at[rows, :], q_ref.at[r], q_sem.at[r])
-
-    def load(r):
-        return pltpu.make_async_copy(kv_hbm.at[:, r], kv_ref.at[r], load_sem.at[r])
-
-    def store(r):
-        return pltpu.make_async_copy(kv_ref.at[r], nc_ref.at[:, r], store_sem.at[r])
-
-    def begin(r, _):
-        q_load(r).start()
-        load(r).start()
+    def row_of(i):
+        return 4 * (i % 4) + i // 4
+
+    def q_load(i):
+        rows = pl.ds(pl.multiple_of(row_of(i) * Q, Q), Q)
+        return pltpu.make_async_copy(q_hbm.at[rows, :], q_ref.at[i], q_sem.at[i])
+
+    def load(i):
+        return pltpu.make_async_copy(kv_hbm.at[:, row_of(i)], kv_ref.at[i], load_sem.at[i])
+
+    def store(i):
+        return pltpu.make_async_copy(kv_ref.at[i], nc_hbm.at[:, row_of(i)], store_sem.at[i])
+
+    def live(i):
+        return jnp.clip(len_ref[row_of(i)] - base, 0, span)
+
+    def begin(i, _):
+        load(i).start()
+
+        @pl.when(i < few)
+        def _():
+            q_load(i).start()
+
         return 0
 
     lax.fori_loop(0, requests, begin, 0)
 
-    def one(r, _):
-        live = jnp.clip(len_ref[r] - base, 0, span)
-        q_load(r).wait()
-        load(r).wait()
-        store(r).start()
-
-        def scores(at):
-            return lax.dot_general(
-                kv_ref[r, 0, pl.ds(at, CHUNK), :],
-                stacked_heads(q_ref[r]),
-                (((1,), (1,)), ((), ())),
-                preferred_element_type=jnp.float32,
-            )
-
-        def folded(s):
-            return jnp.max(s.reshape(CHUNK // 8, 8, width), axis=0)
-
-        def weighted(at, p):
-            values = kv_ref[r, 1, pl.ds(at, CHUNK), :].T
-            values = jnp.concatenate([values, jnp.ones((16, CHUNK), values.dtype)], axis=0)
-            return jnp.dot(values, p, preferred_element_type=jnp.float32)
-
-        def publish(peak, acc):
-            o_ref[r] = acc[:HEAD].astype(o_ref.dtype)
-            st_ref[r, 0:1] = peak
-            st_ref[r, 1:2] = acc[HEAD : HEAD + 1]
-
-        @pl.when(live == 0)
-        def _():
-            publish(jnp.full((1, width), DEAD, jnp.float32), jnp.zeros((HEAD + 16, width), jnp.float32))
-
-        @pl.when(live == span)
-        def _():
-            peak = None
-            for c in range(chunks):
-                s = scores(c * CHUNK)
-                s_ref[pl.ds(c * CHUNK, CHUNK), :] = s
-                peak = folded(s) if peak is None else jnp.maximum(peak, folded(s))
-            peak = jnp.max(peak, axis=0, keepdims=True) * SCALE
-            acc = None
-            for c in range(chunks):
-                p = jnp.exp2(s_ref[pl.ds(c * CHUNK, CHUNK), :] * SCALE - peak).astype(jnp.bfloat16)
-                term = weighted(c * CHUNK, p)
-                acc = term if acc is None else acc + term
-            publish(peak, acc)
-
-        @pl.when((live > 0) & (live < span))
-        def _():
-            used = (live + CHUNK - 1) // CHUNK
-            max_ref[...] = jnp.full_like(max_ref, DEAD)
-            acc_ref[...] = jnp.zeros_like(acc_ref)
-
-            def first(c, _):
-                at = pl.multiple_of(c * CHUNK, CHUNK)
-                row = lax.broadcasted_iota(jnp.int32, (CHUNK, width), 0) + at
-                s = jnp.where(row < live, scores(at), DEAD)
-                s_ref[pl.ds(at, CHUNK), :] = s
-                max_ref[...] = jnp.maximum(max_ref[...], folded(s))
-                return 0
-
-            lax.fori_loop(0, used, first, 0)
-            peak = jnp.max(max_ref[...], axis=0, keepdims=True) * SCALE
-
-            def second(c, _):
-                at = pl.multiple_of(c * CHUNK, CHUNK)
-                row = lax.broadcasted_iota(jnp.int32, (CHUNK, width), 0) + at
-                p = jnp.exp2(s_ref[pl.ds(at, CHUNK), :] * SCALE - peak)
-                p = jnp.where(row < live, p, 0.0).astype(jnp.bfloat16)
-                acc_ref[...] += weighted(at, p)
-                return 0
-
-            lax.fori_loop(0, used, second, 0)
-            publish(peak, acc_ref[...])
-
-        return 0
-
-    lax.fori_loop(0, requests, one, 0)
-
-    def end(r, _):
-        store(r).wait()
+    def listed(i, count):
+        alive = live(i) > 0
+
+        @pl.when(alive)
+        def _():
+            job_ref[count] = i
+
+        @pl.when(jnp.logical_not(alive))
+        def _():
+            o_ref[i] = jnp.zeros(o_ref.shape[1:], o_ref.dtype)
+            st_ref[i, 0:1] = jnp.full((1, st_ref.shape[2]), DEAD, jnp.float32)
+            st_ref[i, 1:2] = jnp.zeros((1, st_ref.shape[2]), jnp.float32)
+
+        return count + jnp.where(alive, 1, 0)
+
+    job_ref[0] = 0
+    jobs = lax.fori_loop(0, few, listed, 0)
+
+    def arrive(i, _):
+        load(i).wait()
+        store(i).start()
+
+        @pl.when(i < few)
+        def _():
+            q_load(i).wait()
+
+        return 0
+
+    def job(n):
+        return job_ref[jnp.clip(n, 0, jnp.maximum(jobs - 1, 0))]
+
+    @pl.when(jobs > 0)
+    def _():
+        first = job(0)
+        lax.fori_loop(0, first + 1, arrive, 0)
+        _, peak = attention_step(
+            None, s_ref.at[0], None, kv_ref.at[first], stacked_heads(q_ref[first]), live(first), s_ref.at[0]
+        )
+        peak_ref[0:1] = peak
+
+        def pair(n, _):
+            for u in range(2):
+                now, later = job(2 * n + u), job(2 * n + u + 1)
+                lax.fori_loop(now + 1, later + 1, arrive, 0)
+                peak = peak_ref[u : u + 1]
+                acc, above = attention_step(
+                    kv_ref.at[now], s_ref.at[u], peak,
+                    kv_ref.at[later], stacked_heads(q_ref[later]), live(later), s_ref.at[1 - u],
+                )
+                publish(o_ref.at[now], st_ref.at[now], peak, acc)
+                peak_ref[1 - u : 2 - u] = above
+            lax.fori_loop(few + 2 * n, few + 2 * n + 2, arrive, 0)
+            return 0
+
+        lax.fori_loop(0, (jobs + 1) // 2, pair, 0)
+
+    lax.fori_loop(jnp.where(jobs > 0, job(jobs) + 1, 0), few, arrive, 0)
+    lax.fori_loop(few + (jobs + 1) // 2 * 2, requests, arrive, 0)
+    outs = [
+        pltpu.make_async_copy(o_ref, o_hbm, out_sem.at[0]),
+        pltpu.make_async_copy(st_ref, st_hbm, out_sem.at[1]),
+    ]
+    for copy in outs:
+        copy.start()
+
+    def end(i, _):
+        store(i).wait()
         return 0
 
     lax.fori_loop(0, requests, end, 0)
+    for copy in outs:
+        copy.wait()
 
 
 def attend(lengths, queries, cache):
     requests, span = cache.shape[1], cache.shape[2]
     wide = queries.shape[1]
     width = wide // HEAD * Q
+    few = requests // 2
+    dma = pltpu.SemaphoreType.DMA
+    far = pl.BlockSpec(memory_space=pl.ANY)
+    o = jax.ShapeDtypeStruct((few, HEAD, width), jnp.bfloat16)
+    st = jax.ShapeDtypeStruct((few, 8, width), jnp.float32)
     return pl.pallas_call(
         attend_kernel,
-        out_shape=(
-            jax.ShapeDtypeStruct((requests, HEAD, width), jnp.bfloat16),
-            jax.ShapeDtypeStruct((requests, 8, width), jnp.float32),
-            jax.ShapeDtypeStruct(cache.shape, cache.dtype),
-        ),
-        in_specs=[
-            pl.BlockSpec(memory_space=pltpu.SMEM),
-            pl.BlockSpec(memory_space=pltpu.HBM),
-            pl.BlockSpec(memory_space=pltpu.HBM),
-        ],
-        out_specs=(
-            pl.BlockSpec(memory_space=pltpu.VMEM),
-            pl.BlockSpec(memory_space=pltpu.VMEM),
-            pl.BlockSpec(memory_space=pltpu.HBM),
-        ),
+        out_shape=(o, st, jax.ShapeDtypeStruct(cache.shape, cache.dtype)),
+        in_specs=[pl.BlockSpec(memory_space=pltpu.SMEM), far, far],
+        out_specs=(far, far, far),
         scratch_shapes=[
-            pltpu.VMEM((requests, Q, wide), jnp.bfloat16),
+            pltpu.VMEM((few, Q, wide), jnp.bfloat16),
             pltpu.VMEM((requests, 2, span, HEAD), jnp.bfloat16),
-            pltpu.VMEM((span, width), jnp.float32),
-            pltpu.VMEM((HEAD + 16, width), jnp.float32),
+            pltpu.VMEM(o.shape, o.dtype),
+            pltpu.VMEM(st.shape, st.dtype),
+            pltpu.VMEM((2, span, width), jnp.float32),
             pltpu.VMEM((8, width), jnp.float32),
-            pltpu.SemaphoreType.DMA((requests,)),
-            pltpu.SemaphoreType.DMA((requests,)),
-            pltpu.SemaphoreType.DMA((requests,)),
+            pltpu.SMEM((few,), jnp.int32),
+            dma((few,)),
+            dma((requests,)),
+            dma((requests,)),
+            dma((2,)),
         ],
         compiler_params=pltpu.CompilerParams(vmem_limit_bytes=60 << 20),
         name="attend",
@@ -266,9 +295,9 @@
 
 
 def join_kernel(
-    o_hbm, st_hbm, q_hbm, dkv_ref, par_ref, path_ref, w_hbm, out_ref, chosen_ref,
-    q_ref, o_ref, st_ref, w_ref, pair_o, pair_st, merge_o, merge_st, acc_ref, run_ref, att, rs_send, rs_recv,
-    q_sem, in_sem, pair_ss, pair_rs, merge_ss, merge_rs, own_ss, relay_ss, pass_ss, att_rs, out_ss, out_rs,
+    len_ref, o_hbm, st_hbm, q_hbm, kv_hbm, dkv_ref, par_ref, path_ref, w_hbm, out_ref, chosen_ref,
+    q_ref, qs_ref, kv_ref, s_ref, peak_ref, o_ref, st_ref, w_ref, pair_o, pair_st, merge_o, merge_st, acc_ref, run_ref, att, rs_send, rs_recv,
+    q_sem, qs_sem, kv_sem, in_sem, pair_ss, pair_rs, merge_ss, merge_rs, own_ss, relay_ss, pass_ss, att_rs, out_ss, out_rs,
 ):
     s, t = lax.axis_index("seq"), lax.axis_index("tp")
     k, c = s // 2, s % 2
@@ -284,16 +313,40 @@
     pl.semaphore_signal(barrier, inc=1, device_id={"seq": partner}, device_id_type=MESH)
     for d in range(1, tps):
         pl.semaphore_signal(barrier, inc=1, device_id={"tp": (t + d) % tps}, device_id_type=MESH)
+    few, span = o_hbm.shape[0], kv_ref.shape[2]
+    jobs = jnp.where(k < 4, kv_ref.shape[0], kv_ref.shape[0] // 2)
+
+    def place(i):
+        return 3 - i // 4, i % 4
+
+    def row_of(i):
+        tenant, turn = place(i)
+        return 4 * turn + tenant
+
+    def live(i):
+        return jnp.clip(len_ref[row_of(i)] - s * span, 0, span)
+
+    def qs_load(i):
+        rows = pl.ds(pl.multiple_of(row_of(i) * Q, Q), Q)
+        return pltpu.make_async_copy(q_hbm.at[rows, :], qs_ref.at[i], qs_sem.at[i])
+
+    def kv_load(i):
+        return pltpu.make_async_copy(kv_hbm.at[:, row_of(i)], kv_ref.at[i], kv_sem.at[i])
+
     q_copy = pltpu.make_async_copy(q_hbm.at[pl.ds(pl.multiple_of(s * Q, Q), Q), :], q_ref, q_sem)
     q_copy.start()
+
+    def start_load(i, _):
+        qs_load(i).start()
+        kv_load(i).start()
+        return 0
+
+    lax.fori_loop(0, jobs, start_load, 0)
     w_copy = pltpu.make_async_copy(w_hbm, w_ref, in_sem.at[0])
-    o_copy = pltpu.make_async_copy(o_hbm, o_ref, in_sem.at[1])
-    st_copy = pltpu.make_async_copy(st_hbm, st_ref, in_sem.at[2])
+    o_copy = pltpu.make_async_copy(o_hbm, o_ref.at[pl.ds(0, few)], in_sem.at[1])
+    st_copy = pltpu.make_async_copy(st_hbm, st_ref.at[pl.ds(0, few)], in_sem.at[2])
     for copy in (o_copy, st_copy, w_copy):
         copy.start()
-    o_copy.wait()
-    st_copy.wait()
-    pl.semaphore_wait(barrier, chips + tps - 1)
 
     def send(src, dst, ss, rs, **where):
         return pltpu.make_async_remote_copy(
@@ -301,7 +354,7 @@
         )
 
     def pair_copies(j):
-        r = 2 * j + 1 - c
+        r = 4 * (2 * (j % 2) + 1 - c) + j // 2
         return (
             send(o_ref.at[r], pair_o.at[j], pair_ss.at[j, 0], pair_rs.at[j, 0], seq=partner),
             send(st_ref.at[r], pair_st.at[j], pair_ss.at[j, 1], pair_rs.at[j, 1], seq=partner),
@@ -333,21 +386,6 @@
 
     def reach_of(j, parity):
         return (1 + 3 * (j % 2)) * (1 + parity)
-
-    def in_order(i):
-        return (k // 2 * 2 + 2 * (i % 4) + i // 4) % chips
-
-    def start_pair(i, _):
-        j = in_order(i)
-
-        @pl.when(k < reach_of(j, 1 - c))
-        def _():
-            for copy in pair_copies(j):
-                copy.start()
-
-        return 0
-
-    lax.fori_loop(0, chips, start_pair, 0)
 
     node = lax.broadcasted_iota(jnp.int32, (Q, Q), 0)
     other = lax.broadcasted_iota(jnp.int32, (Q, Q), 1)
@@ -370,30 +408,90 @@
     run_ref[1:2] = jnp.sum(weights, axis=0, keepdims=True)
     acc_ref[...] = jnp.dot(dkv_ref[1].T, weights.astype(jnp.bfloat16), preferred_element_type=jnp.float32)
 
-    def combine(i, _):
-        j = in_order(i)
-        r = 2 * j + c
-
-        @pl.when(k < reach_of(j, c))
-        def _():
-            for copy in pair_copies(j):
-                copy.wait_recv()
-            peak, total, a, b = folded_parts(
-                (st_ref[r, 0:1], st_ref[r, 1:2]), (pair_st[j, 0:1], pair_st[j, 1:2])
+    def combine(tenant, turn):
+        j = 2 * turn + tenant // 2
+        r = 4 * tenant + turn
+        for copy in pair_copies(j):
+            copy.wait_recv()
+        peak, total, a, b = folded_parts((st_ref[r, 0:1], st_ref[r, 1:2]), (pair_st[j, 0:1], pair_st[j, 1:2]))
+        mixed = o_ref[r].astype(jnp.float32) * a + pair_o[j].astype(jnp.float32) * b
+        pair_o[j] = mixed.astype(jnp.bfloat16)
+        pair_st[j, 0:1] = peak
+        pair_st[j, 1:2] = total
+
+        @pl.when(j != k)
+        def _():
+            for copy in merge_copies(j):
+                copy.start()
+
+    def combine_all(tenant):
+        def each(turn, _):
+            combine(tenant, (turn + k // 2) % 4)
+            return 0
+
+        @pl.when((tenant % 2 == c) & (k < 2**tenant))
+        def _():
+            lax.fori_loop(0, 4, each, 0)
+
+    def start_pair(tenant, turn):
+        @pl.when((tenant % 2 != c) & (k < reach_of(tenant // 2, tenant % 2)))
+        def _():
+            for copy in pair_copies(2 * turn + tenant // 2):
+                copy.start()
+
+    qs_load(0).wait()
+    kv_load(0).wait()
+    _, above = attention_step(
+        None, s_ref.at[0], None, kv_ref.at[0], stacked_heads(qs_ref[0]), live(0), s_ref.at[0]
+    )
+    peak_ref[0:1] = above
+    o_copy.wait()
+    st_copy.wait()
+    pl.semaphore_wait(barrier, chips + tps - 1)
+    for tenant in range(2):
+        for turn in range(4):
+            start_pair(tenant, turn)
+
+    def attend_pair(n, _):
+        for u in range(2):
+            now = 2 * n + u
+            later = jnp.where(now + 1 < jobs, now + 1, 0)
+
+            @pl.when(now + 1 < jobs)
+            def _():
+                qs_load(later).wait()
+                kv_load(later).wait()
+
+            peak = peak_ref[u : u + 1]
+            acc, above = attention_step(
+                kv_ref.at[now], s_ref.at[u], peak,
+                kv_ref.at[later], stacked_heads(qs_ref[later]), live(later), s_ref.at[1 - u],
             )
-            mixed = o_ref[r].astype(jnp.float32) * a + pair_o[j].astype(jnp.float32) * b
-            pair_o[j] = mixed.astype(jnp.bfloat16)
-            pair_st[j, 0:1] = peak
-            pair_st[j, 1:2] = total
-
-            @pl.when(j != k)
-            def _():
-                for copy in merge_copies(j):
-                    copy.start()
-
-        return 0
-
-    lax.fori_loop(0, chips, combine, 0)
+            tenant, turn = place(now)
+            publish(o_ref.at[4 * tenant + turn], st_ref.at[4 * tenant + turn], peak, acc)
+            peak_ref[1 - u : 2 - u] = above
+            start_pair(tenant, turn)
+
+        @pl.when(n == 1)
+        def _():
+            combine_all(0)
+            combine_all(1)
+
+        @pl.when(n == 2)
+        def _():
+            combine_all(3)
+
+        return 0
+
+    lax.fori_loop(0, jobs // 2, attend_pair, 0)
+
+    @pl.when(k < 4)
+    def _():
+        combine_all(2)
+
+    @pl.when(k >= 4)
+    def _():
+        combine_all(3)
 
     def absorb(o, st):
         peak, total, a, b = folded_parts((run_ref[0:1], run_ref[1:2]), (st[0:1], st[1:2]))
@@ -520,8 +618,9 @@
         copy.wait_send()
 
 
-def join(o, st, queries, draft_kv, parents, path, out_weight, chips, tps):
-    requests, _, width = o.shape
+def join(lengths, o, st, queries, cache, draft_kv, parents, path, out_weight, chips, tps):
+    requests, span = cache.shape[1], cache.shape[2]
+    few, _, width = o.shape
     wide, columns = queries.shape[1], out_weight.shape[1]
     dma = pltpu.SemaphoreType.DMA
     whole, far = pl.BlockSpec(memory_space=pltpu.VMEM), pl.BlockSpec(memory_space=pl.ANY)
@@ -531,12 +630,16 @@
             jax.ShapeDtypeStruct((queries.shape[0] // tps, columns), jnp.bfloat16),
             jax.ShapeDtypeStruct((requests, 4 * ACC, HEAD), jnp.bfloat16),
         ),
-        in_specs=[far, far, far, whole, whole, whole, far],
+        in_specs=[pl.BlockSpec(memory_space=pltpu.SMEM), far, far, far, far, whole, whole, whole, far],
         out_specs=(whole, whole),
         scratch_shapes=[
             pltpu.VMEM((Q, wide), jnp.bfloat16),
-            pltpu.VMEM(o.shape, o.dtype),
-            pltpu.VMEM(st.shape, st.dtype),
+            pltpu.VMEM((requests // 2, Q, wide), jnp.bfloat16),
+            pltpu.VMEM((requests // 2, 2, span, HEAD), jnp.bfloat16),
+            pltpu.VMEM((2, span, width), jnp.float32),
+            pltpu.VMEM((8, width), jnp.float32),
+            pltpu.VMEM((requests, HEAD, width), o.dtype),
+            pltpu.VMEM((requests, 8, width), st.dtype),
             pltpu.VMEM(out_weight.shape, out_weight.dtype),
             pltpu.VMEM((chips, HEAD, width), jnp.bfloat16),
             pltpu.VMEM((chips, 8, width), jnp.float32),
@@ -548,6 +651,8 @@
             pltpu.VMEM((tps, 2 * Q, columns), jnp.bfloat16),
             pltpu.VMEM((tps, 2 * Q, columns), jnp.bfloat16),
             dma,
+            dma((requests // 2,)),
+            dma((requests // 2,)),
             dma((3,)),
             dma((chips, 2)),
             dma((chips, 2)),
@@ -564,7 +669,7 @@
             collective_id=0, has_side_effects=True, vmem_limit_bytes=60 << 20
         ),
         name="join",
-    )(o, st, queries, draft_kv, parents, path, out_weight)
+    )(lengths, o, st, queries, cache, draft_kv, parents, path, out_weight)
 
 
 def solution(mesh):
@@ -572,7 +677,7 @@
 
     def local(queries, cache, draft_kv, out_weight, lengths, parents, path, accepted):
         o, st, new_cache = attend(lengths, queries, cache)
-        attn, chosen = join(o, st, queries, draft_kv, parents, path.T, out_weight, chips, tps)
+        attn, chosen = join(lengths, o, st, queries, cache, draft_kv, parents, path.T, out_weight, chips, tps)
         return commit(lengths, accepted, chosen, attn, new_cache)
 
     return jax.shard_map(

time: 82.6 us -> 74.7 us (0.904)
  the two profiles are of different devices: /device:TPU:114 before, /device:TPU:47 now
where the time goes in v4:
time: 74.7 us; the launch traced here: 74.4 us
  Pallas kernels  73.8 us (99%)
    pallas_call x1, Pallas kernels, join(): pl.pallas_call(join_kernel, out_shape=(jax.ShapeDtypeStruct((queries.shap...  61.4 us
    pallas_call x1, Pallas kernels, attend(): pl.pallas_call(attend_kernel, out_shape=(o, st, jax.ShapeDtypeStruct(cach...  8.77 us
    pallas_call x1, Pallas kernels, commit(): pl.pallas_call(commit_kernel, out_shape=(jax.ShapeDtypeStruct(attn.shape,...  3.66 us

profile of v4, /device:TPU:47, one launch (start us, length us, event | category | flops | bytes accessed | tf_op | source)
XLA Modules:
  0.0 74.4 jit_solution(16473537105805677090)
XLA Ops:
  0.6 8.8 %attend.1 = (bf16[8,128,512]{2,1,0:T(8,128)(2,1)}, f32[8,8,512]{2,1,0:T(8,128)}, bf16[2,16,1024,128]{3,2,1,0:T(8,128)(2,1)}) custom-call(s32[16]{0:T(128)} %len_ref.5, bf16[1024,1024]{1,0:T(8,128)(2,1)} %q_hbm.3, bf16[2,16,1024,128]{3,2,1,0:T(8,128)(2,1)} %kv_hbm.3), custom_call_target="tpu_custom_call" | custom-call | tf_op jit(solution)/shard_map/attend/pallas_call | solution.py:177
  9.4 61.4 %join.1 = (bf16[128,512]{1,0:T(8,128)(2,1)}, bf16[16,32,128]{2,1,0:T(8,128)(2,1)}) custom-call(s32[16]{0:T(128)} %len_ref.5, bf16[8,128,512]{2,1,0:T(8,128)(2,1)} %get-tuple-element.7.o_hbm, f32[8,8,512]{2,1,0:T(8,128)} %get-tuple-element.8.st_hbm, bf16[1024,1024]{1,0:T(8,128)(2,1)} %q_hbm.3, bf16[2,16,1024,128]{3,2,1,0:T(8,128)(2,1)} %kv_hbm.3, ...), custom_call_target="tpu_custom_call" | custom-call | tf_op jit(solution)/shard_map/join/pallas_call | solution.py:627
  70.8 3.7 %commit.1 = (bf16[128,512]{1,0:T(8,128)(2,1)}, bf16[2,16,1024,128]{3,2,1,0:T(8,128)(2,1)}) custom-call(s32[16]{0:T(128)} %len_ref.5, s32[16]{0:T(128)} %acc_ref.1, bf16[16,32,128]{2,1,0:T(8,128)(2,1)} %get-tuple-element.9.chosen_ref, bf16[128,512]{1,0:T(8,128)(2,1)} %get-tuple-element.10.attn_ref, ...), custom_call_target="tpu_custom_call", output_to_operand_aliasing={{1}: (4, {})} | custom-call | tf_op jit(solution)/shard_map/commit/pallas_call | solution.py:271

commit v5 on v4

--- a/solution.py
+++ b/solution.py
@@ -296,12 +296,13 @@
 
 def join_kernel(
     len_ref, o_hbm, st_hbm, q_hbm, kv_hbm, dkv_ref, par_ref, path_ref, w_hbm, out_ref, chosen_ref,
-    q_ref, qs_ref, kv_ref, s_ref, peak_ref, o_ref, st_ref, w_ref, pair_o, pair_st, merge_o, merge_st, acc_ref, run_ref, att, rs_send, rs_recv,
-    q_sem, qs_sem, kv_sem, in_sem, pair_ss, pair_rs, merge_ss, merge_rs, own_ss, relay_ss, pass_ss, att_rs, out_ss, out_rs,
+    q_ref, qs_ref, kv_ref, s_ref, peak_ref, o_ref, st_ref, w_ref, pair_o, pair_st, merge_o, merge_st, acc_ref, run_ref, att, rs_send, rs_recv, half_ref,
+    q_sem, qs_sem, kv_sem, in_sem, pair_ss, pair_rs, merge_ss, merge_rs, own_ss, pass_ss, att_rs, out_ss, out_rs, half_sem,
 ):
     s, t = lax.axis_index("seq"), lax.axis_index("tp")
     k, c = s // 2, s % 2
     y, z = k // 4, k % 4
+    lx, across = t % 4, (t + 4) % 8
     chips, tps = pair_o.shape[0], rs_send.shape[0]
     partner = 2 * k + 1 - c
     width = o_ref.shape[2]
@@ -357,19 +358,19 @@
         r = 4 * (2 * (j % 2) + 1 - c) + j // 2
         return (
             send(o_ref.at[r], pair_o.at[j], pair_ss.at[j, 0], pair_rs.at[j, 0], seq=partner),
-            send(st_ref.at[r], pair_st.at[j], pair_ss.at[j, 1], pair_rs.at[j, 1], seq=partner),
+            send(st_ref.at[r, pl.ds(0, 2)], pair_st.at[j, pl.ds(0, 2)], pair_ss.at[j, 1], pair_rs.at[j, 1], seq=partner),
         )
 
     def merge_copies(j):
         return (
             send(pair_o.at[j], merge_o.at[k], merge_ss.at[j, 0], merge_rs.at[k, 0], seq=2 * j + c),
-            send(pair_st.at[j], merge_st.at[k], merge_ss.at[j, 1], merge_rs.at[k, 1], seq=2 * j + c),
+            send(pair_st.at[j, pl.ds(0, 2)], merge_st.at[k, pl.ds(0, 2)], merge_ss.at[j, 1], merge_rs.at[k, 1], seq=2 * j + c),
         )
 
     def merge_arrival(i):
         return (
             send(pair_o.at[i], merge_o.at[i], merge_ss.at[i, 0], merge_rs.at[i, 0], seq=partner),
-            send(pair_st.at[i], merge_st.at[i], merge_ss.at[i, 1], merge_rs.at[i, 1], seq=partner),
+            send(pair_st.at[i, pl.ds(0, 2)], merge_st.at[i, pl.ds(0, 2)], merge_ss.at[i, 1], merge_rs.at[i, 1], seq=partner),
         )
 
     def pass_on(slot, ss, where):
@@ -378,8 +379,16 @@
     def ring(d):
         return 2 * (y * 4 + (z + d) % 4) + c
 
+    def far_ring(d):
+        return 2 * ((1 - y) * 4 + (z + d) % 4) + c
+
     def out_copy(g):
-        return send(rs_send.at[g], rs_recv.at[t], out_ss.at[g], out_rs.at[t], tp=g)
+        slot = jnp.where(g % 2 == 1, t, g // 4 * 4 + lx)
+        where = jnp.where(g % 2 == 1, g, t // 4 * 4 + g % 4)
+        return send(rs_send.at[g], rs_recv.at[slot], out_ss.at[g], out_rs.at[slot], tp=where)
+
+    def leaves(g):
+        return jnp.where(g % 2 == 1, g != t, g % 4 != lx)
 
     def out_arrival(i):
         return send(rs_send.at[i], rs_recv.at[i], out_ss.at[i], out_rs.at[i], seq=partner)
@@ -445,14 +454,7 @@
         None, s_ref.at[0], None, kv_ref.at[0], stacked_heads(qs_ref[0]), live(0), s_ref.at[0]
     )
     peak_ref[0:1] = above
-    o_copy.wait()
-    st_copy.wait()
-    pl.semaphore_wait(barrier, chips + tps - 1)
-    for tenant in range(2):
-        for turn in range(4):
-            start_pair(tenant, turn)
-
-    def attend_pair(n, _):
+    def attend_two(n):
         for u in range(2):
             now = 2 * n + u
             later = jnp.where(now + 1 < jobs, now + 1, 0)
@@ -470,7 +472,24 @@
             tenant, turn = place(now)
             publish(o_ref.at[4 * tenant + turn], st_ref.at[4 * tenant + turn], peak, acc)
             peak_ref[1 - u : 2 - u] = above
+
+    attend_two(0)
+    o_copy.wait()
+    st_copy.wait()
+    pl.semaphore_wait(barrier, chips + tps - 1)
+    for tenant in range(2):
+        for turn in range(4):
             start_pair(tenant, turn)
+
+    def start_two(n):
+        for u in range(2):
+            start_pair(*place(2 * n + u))
+
+    start_two(0)
+
+    def attend_pair(n, _):
+        attend_two(n)
+        start_two(n)
 
         @pl.when(n == 1)
         def _():
@@ -483,7 +502,7 @@
 
         return 0
 
-    lax.fori_loop(0, jobs // 2, attend_pair, 0)
+    lax.fori_loop(1, jobs // 2, attend_pair, 0)
 
     @pl.when(k < 4)
     def _():
@@ -531,6 +550,7 @@
     own = [pass_on(s, own_ss.at[0], 2 * twin + c)]
     own += [pass_on(s, own_ss.at[d], ring(d)) for d in (1, 3, 2)]
     own += [pass_on(s, own_ss.at[4], partner)]
+    own += [pass_on(s, own_ss.at[4 + d], far_ring(d)) for d in (1, 3, 2)]
     for copy in own:
         copy.start()
 
@@ -539,9 +559,6 @@
 
     def forward(g):
         return pass_on(2 * g + c, pass_ss.at[g], partner)
-
-    def relays():
-        return [pass_on(2 * twin + c, relay_ss.at[d], ring(d)) for d in (1, 3, 2)]
 
     def arrival(slot):
         return pass_on(slot, own_ss.at[0], partner)
@@ -557,7 +574,7 @@
         )
         rs_send[g] = jnp.dot(rows, w_ref[...], preferred_element_type=jnp.float32).astype(jnp.bfloat16)
 
-        @pl.when(g != t)
+        @pl.when(leaves(g))
         def _():
             out_copy(g).start()
 
@@ -568,11 +585,6 @@
         def _():
             arrival(2 * g + c).wait_recv()
             forward(g).start()
-
-        @pl.when(g == twin)
-        def _():
-            for copy in relays():
-                copy.start()
 
         @pl.when(i > 0)
         def _():
@@ -584,12 +596,30 @@
     lax.fori_loop(0, chips, spread_on, 0)
     project(group(chips - 1))
 
-    total = rs_send[t].astype(jnp.float32)
-    for d in range(1, tps):
-        i = (t + d) % tps
-        out_arrival(i).wait_recv()
-        total = total + rs_recv[i].astype(jnp.float32)
-    out_ref[...] = total.astype(out_ref.dtype)
+    def gathered(g, slots):
+        total = rs_send[g].astype(jnp.float32)
+        for i in slots:
+            out_arrival(i).wait_recv()
+            total = total + rs_recv[i].astype(jnp.float32)
+        return total
+
+    def row_slots(g):
+        return [g // 4 * 4 + (lx + d) % 4 for d in range(1, 4)]
+
+    swap = send(half_ref.at[0], half_ref.at[1], half_sem.at[0], half_sem.at[1], tp=across)
+
+    @pl.when(t % 2 == 0)
+    def _():
+        half_ref[0] = gathered(across, row_slots(across)).astype(jnp.bfloat16)
+        swap.start()
+        total = gathered(t, row_slots(t))
+        swap.wait()
+        out_ref[...] = (total + half_ref[1].astype(jnp.float32)).astype(out_ref.dtype)
+
+    @pl.when(t % 2 == 1)
+    def _():
+        out_ref[...] = gathered(t, [(t + d) % tps for d in range(1, tps)]).astype(out_ref.dtype)
+
     chosen_ref[...] = att[:, width:]
 
     def finish_pair(j, _):
@@ -607,14 +637,14 @@
         def _():
             forward(j).wait_send()
 
-        @pl.when(j != t)
+        @pl.when(leaves(j))
         def _():
             out_copy(j).wait_send()
 
         return 0
 
     lax.fori_loop(0, chips, finish_pair, 0)
-    for copy in own + relays():
+    for copy in own:
         copy.wait_send()
 
 
@@ -650,6 +680,7 @@
             pltpu.VMEM((requests, width + 4 * ACC, HEAD), jnp.bfloat16),
             pltpu.VMEM((tps, 2 * Q, columns), jnp.bfloat16),
             pltpu.VMEM((tps, 2 * Q, columns), jnp.bfloat16),
+            pltpu.VMEM((2, 2 * Q, columns), jnp.bfloat16),
             dma,
             dma((requests // 2,)),
             dma((requests // 2,)),
@@ -658,12 +689,12 @@
             dma((chips, 2)),
             dma((chips, 2)),
             dma((chips, 2)),
-            dma((5,)),
-            dma((4,)),
+            dma((8,)),
             dma((chips,)),
             dma((requests,)),
             dma((tps,)),
             dma((tps,)),
+            dma((2,)),
         ],
         compiler_params=pltpu.CompilerParams(
             collective_id=0, has_side_effects=True, vmem_limit_bytes=60 << 20

time: 74.7 us -> 69 us (0.924)
  Pallas kernels: 73.8 us -> 68.1 us
    pallas_call x1, Pallas kernels: 61.4 us -> 56 us  [join(): pl.pallas_call(join_kernel, out_shape=(jax.ShapeDtypeStruct((queries.shap...]
where the time goes in v5:
time: 69 us; the launch traced here: 68.8 us
  Pallas kernels  68.1 us (99%)
    pallas_call x1, Pallas kernels, join(): pl.pallas_call(join_kernel, out_shape=(jax.ShapeDtypeStruct((queries.shap...  56 us
    pallas_call x1, Pallas kernels, attend(): pl.pallas_call(attend_kernel, out_shape=(o, st, jax.ShapeDtypeStruct(cach...  8.33 us
    pallas_call x1, Pallas kernels, commit(): pl.pallas_call(commit_kernel, out_shape=(jax.ShapeDtypeStruct(attn.shape,...  3.8 us

profile of v5, /device:TPU:47, one launch (start us, length us, event | category | flops | bytes accessed | tf_op | source)
XLA Modules:
  0.0 68.8 jit_solution(9089875837102169095)
XLA Ops:
  0.6 8.3 %attend.1 = (bf16[8,128,512]{2,1,0:T(8,128)(2,1)}, f32[8,8,512]{2,1,0:T(8,128)}, bf16[2,16,1024,128]{3,2,1,0:T(8,128)(2,1)}) custom-call(s32[16]{0:T(128)} %len_ref.5, bf16[1024,1024]{1,0:T(8,128)(2,1)} %q_hbm.3, bf16[2,16,1024,128]{3,2,1,0:T(8,128)(2,1)} %kv_hbm.3), custom_call_target="tpu_custom_call" | custom-call | tf_op jit(solution)/shard_map/attend/pallas_call | solution.py:177
  9.0 56.0 %join.1 = (bf16[128,512]{1,0:T(8,128)(2,1)}, bf16[16,32,128]{2,1,0:T(8,128)(2,1)}) custom-call(s32[16]{0:T(128)} %len_ref.5, bf16[8,128,512]{2,1,0:T(8,128)(2,1)} %get-tuple-element.7.o_hbm, f32[8,8,512]{2,1,0:T(8,128)} %get-tuple-element.8.st_hbm, bf16[1024,1024]{1,0:T(8,128)(2,1)} %q_hbm.3, bf16[2,16,1024,128]{3,2,1,0:T(8,128)(2,1)} %kv_hbm.3, ...), custom_call_target="tpu_custom_call" | custom-call | tf_op jit(solution)/shard_map/join/pallas_call | solution.py:657
  65.0 3.8 %commit.1 = (bf16[128,512]{1,0:T(8,128)(2,1)}, bf16[2,16,1024,128]{3,2,1,0:T(8,128)(2,1)}) custom-call(s32[16]{0:T(128)} %len_ref.5, s32[16]{0:T(128)} %acc_ref.1, bf16[16,32,128]{2,1,0:T(8,128)(2,1)} %get-tuple-element.9.chosen_ref, bf16[128,512]{1,0:T(8,128)(2,1)} %get-tuple-element.10.attn_ref, ...), custom_call_target="tpu_custom_call", output_to_operand_aliasing={{1}: (4, {})} | custom-call | tf_op jit(solution)/shard_map/commit/pallas_call | solution.py:271

commit v6 on v5

--- a/solution.py
+++ b/solution.py
@@ -56,176 +56,28 @@
     st[1:2] = acc[HEAD : HEAD + 1]
 
 
-def attend_kernel(
-    len_ref, q_hbm, kv_hbm, o_hbm, st_hbm, nc_hbm,
-    q_ref, kv_ref, o_ref, st_ref, s_ref, peak_ref, job_ref, q_sem, load_sem, store_sem, out_sem,
+def commit_kernel(
+    len_ref, acc_ref, chosen_ref, attn_ref, kv_ref, out_ref, nc_ref, win_ref, store_sem, win_sem
 ):
     requests, span = kv_ref.shape[0], kv_ref.shape[2]
-    few = o_ref.shape[0]
     base = lax.axis_index("seq") * span
 
-    def row_of(i):
-        return 4 * (i % 4) + i // 4
-
-    def q_load(i):
-        rows = pl.ds(pl.multiple_of(row_of(i) * Q, Q), Q)
-        return pltpu.make_async_copy(q_hbm.at[rows, :], q_ref.at[i], q_sem.at[i])
-
-    def load(i):
-        return pltpu.make_async_copy(kv_hbm.at[:, row_of(i)], kv_ref.at[i], load_sem.at[i])
-
-    def store(i):
-        return pltpu.make_async_copy(kv_ref.at[i], nc_hbm.at[:, row_of(i)], store_sem.at[i])
-
-    def live(i):
-        return jnp.clip(len_ref[row_of(i)] - base, 0, span)
-
-    def begin(i, _):
-        load(i).start()
-
-        @pl.when(i < few)
-        def _():
-            q_load(i).start()
-
-        return 0
-
-    lax.fori_loop(0, requests, begin, 0)
-
-    def listed(i, count):
-        alive = live(i) > 0
-
-        @pl.when(alive)
-        def _():
-            job_ref[count] = i
-
-        @pl.when(jnp.logical_not(alive))
-        def _():
-            o_ref[i] = jnp.zeros(o_ref.shape[1:], o_ref.dtype)
-            st_ref[i, 0:1] = jnp.full((1, st_ref.shape[2]), DEAD, jnp.float32)
-            st_ref[i, 1:2] = jnp.zeros((1, st_ref.shape[2]), jnp.float32)
-
-        return count + jnp.where(alive, 1, 0)
-
-    job_ref[0] = 0
-    jobs = lax.fori_loop(0, few, listed, 0)
-
-    def arrive(i, _):
-        load(i).wait()
-        store(i).start()
-
-        @pl.when(i < few)
-        def _():
-            q_load(i).wait()
-
-        return 0
-
-    def job(n):
-        return job_ref[jnp.clip(n, 0, jnp.maximum(jobs - 1, 0))]
-
-    @pl.when(jobs > 0)
-    def _():
-        first = job(0)
-        lax.fori_loop(0, first + 1, arrive, 0)
-        _, peak = attention_step(
-            None, s_ref.at[0], None, kv_ref.at[first], stacked_heads(q_ref[first]), live(first), s_ref.at[0]
-        )
-        peak_ref[0:1] = peak
-
-        def pair(n, _):
-            for u in range(2):
-                now, later = job(2 * n + u), job(2 * n + u + 1)
-                lax.fori_loop(now + 1, later + 1, arrive, 0)
-                peak = peak_ref[u : u + 1]
-                acc, above = attention_step(
-                    kv_ref.at[now], s_ref.at[u], peak,
-                    kv_ref.at[later], stacked_heads(q_ref[later]), live(later), s_ref.at[1 - u],
-                )
-                publish(o_ref.at[now], st_ref.at[now], peak, acc)
-                peak_ref[1 - u : 2 - u] = above
-            lax.fori_loop(few + 2 * n, few + 2 * n + 2, arrive, 0)
-            return 0
-
-        lax.fori_loop(0, (jobs + 1) // 2, pair, 0)
-
-    lax.fori_loop(jnp.where(jobs > 0, job(jobs) + 1, 0), few, arrive, 0)
-    lax.fori_loop(few + (jobs + 1) // 2 * 2, requests, arrive, 0)
-    outs = [
-        pltpu.make_async_copy(o_ref, o_hbm, out_sem.at[0]),
-        pltpu.make_async_copy(st_ref, st_hbm, out_sem.at[1]),
-    ]
-    for copy in outs:
-        copy.start()
-
-    def end(i, _):
-        store(i).wait()
-        return 0
-
-    lax.fori_loop(0, requests, end, 0)
-    for copy in outs:
-        copy.wait()
-
-
-def attend(lengths, queries, cache):
-    requests, span = cache.shape[1], cache.shape[2]
-    wide = queries.shape[1]
-    width = wide // HEAD * Q
-    few = requests // 2
-    dma = pltpu.SemaphoreType.DMA
-    far = pl.BlockSpec(memory_space=pl.ANY)
-    o = jax.ShapeDtypeStruct((few, HEAD, width), jnp.bfloat16)
-    st = jax.ShapeDtypeStruct((few, 8, width), jnp.float32)
-    return pl.pallas_call(
-        attend_kernel,
-        out_shape=(o, st, jax.ShapeDtypeStruct(cache.shape, cache.dtype)),
-        in_specs=[pl.BlockSpec(memory_space=pltpu.SMEM), far, far],
-        out_specs=(far, far, far),
-        scratch_shapes=[
-            pltpu.VMEM((few, Q, wide), jnp.bfloat16),
-            pltpu.VMEM((requests, 2, span, HEAD), jnp.bfloat16),
-            pltpu.VMEM(o.shape, o.dtype),
-            pltpu.VMEM(st.shape, st.dtype),
-            pltpu.VMEM((2, span, width), jnp.float32),
-            pltpu.VMEM((8, width), jnp.float32),
-            pltpu.SMEM((few,), jnp.int32),
-            dma((few,)),
-            dma((requests,)),
-            dma((requests,)),
-            dma((2,)),
-        ],
-        compiler_params=pltpu.CompilerParams(vmem_limit_bytes=60 << 20),
-        name="attend",
-    )(lengths, queries, cache)
-
-
-def commit_kernel(
-    len_ref, acc_ref, chosen_ref, attn_ref, nc_in, out_ref, nc_ref, win_ref, load_sem, store_sem
-):
-    requests, span = nc_ref.shape[1], nc_ref.shape[2]
-    base = lax.axis_index("seq") * span
+    def held(r):
+        return (3 - r % 4) * 4 + r // 4
 
     def place(r):
         off = len_ref[r] - base
         hit = (off + acc_ref[r] > 0) & (off < span)
-        start = pl.multiple_of(jnp.clip(off // 16 * 16, 0, span - WINDOW), 16)
-        return off, hit, start
-
-    def load(r, start):
-        return pltpu.make_async_copy(
-            nc_ref.at[:, r, pl.ds(start, WINDOW), :], win_ref.at[r], load_sem.at[r]
-        )
-
-    def store(r, start):
-        return pltpu.make_async_copy(
-            win_ref.at[r], nc_ref.at[:, r, pl.ds(start, WINDOW), :], store_sem.at[r]
-        )
+        return off, hit, pl.multiple_of(jnp.clip(off // 16 * 16, 0, span - WINDOW), 16)
+
+    def store(r):
+        return pltpu.make_async_copy(kv_ref.at[held(r)], nc_ref.at[:, r], store_sem.at[r])
+
+    def patch(r, start):
+        return pltpu.make_async_copy(win_ref.at[r], nc_ref.at[:, r, pl.ds(start, WINDOW), :], win_sem.at[r])
 
     def begin(r, _):
-        off, hit, start = place(r)
-
-        @pl.when(hit)
-        def _():
-            load(r, start).start()
-
+        store(r).start()
         return 0
 
     def change(r, _):
@@ -238,25 +90,33 @@
             pick = jnp.where(row == node, 1.0, 0.0).astype(jnp.bfloat16)
             slot = lax.broadcasted_iota(jnp.int32, (WINDOW, HEAD), 0) + (start - off)
             fresh = (slot >= 0) & (slot < acc_ref[r])
-            load(r, start).wait()
             for x in range(2):
                 rows = jnp.dot(
                     pick,
                     chosen_ref[r, 2 * ACC * x : 2 * ACC * (x + 1)],
                     preferred_element_type=jnp.float32,
                 )
-                old = win_ref[r, x].astype(jnp.float32)
+                old = kv_ref[held(r), x, pl.ds(start, WINDOW), :].astype(jnp.float32)
                 win_ref[r, x] = jnp.where(fresh, rows, old).astype(jnp.bfloat16)
-            store(r, start).start()
 
         return 0
 
     def end(r, _):
         off, hit, start = place(r)
+        store(r).wait()
 
         @pl.when(hit)
         def _():
-            store(r, start).wait()
+            patch(r, start).start()
+
+        return 0
+
+    def close(r, _):
+        off, hit, start = place(r)
+
+        @pl.when(hit)
+        def _():
+            patch(r, start).wait()
 
         return 0
 
@@ -264,28 +124,28 @@
     out_ref[...] = attn_ref[...]
     lax.fori_loop(0, requests, change, 0)
     lax.fori_loop(0, requests, end, 0)
-
-
-def commit(lengths, accepted, chosen, attn, new_cache):
-    requests = new_cache.shape[1]
+    lax.fori_loop(0, requests, close, 0)
+
+
+def commit(lengths, accepted, chosen, attn, held, shape):
+    requests = shape[1]
+    near, far = pl.BlockSpec(memory_space=pltpu.VMEM), pl.BlockSpec(memory_space=pl.ANY)
     return pl.pallas_call(
         commit_kernel,
         out_shape=(
             jax.ShapeDtypeStruct(attn.shape, attn.dtype),
-            jax.ShapeDtypeStruct(new_cache.shape, new_cache.dtype),
+            jax.ShapeDtypeStruct(shape, held.dtype),
         ),
-        in_specs=[pl.BlockSpec(memory_space=pltpu.SMEM)] * 2
-        + [pl.BlockSpec(memory_space=pltpu.VMEM)] * 2
-        + [pl.BlockSpec(memory_space=pl.ANY)],
-        out_specs=(pl.BlockSpec(memory_space=pltpu.VMEM), pl.BlockSpec(memory_space=pl.ANY)),
+        in_specs=[pl.BlockSpec(memory_space=pltpu.SMEM)] * 2 + [near] * 3,
+        out_specs=(near, far),
         scratch_shapes=[
             pltpu.VMEM((requests, 2, WINDOW, HEAD), jnp.bfloat16),
             pltpu.SemaphoreType.DMA((requests,)),
             pltpu.SemaphoreType.DMA((requests,)),
         ],
-        input_output_aliases={4: 1},
+        compiler_params=pltpu.CompilerParams(vmem_limit_bytes=40 << 20),
         name="commit",
-    )(lengths, accepted, chosen, attn, new_cache)
+    )(lengths, accepted, chosen, attn, held)
 
 
 def folded_parts(first, second):
@@ -295,8 +155,8 @@
 
 
 def join_kernel(
-    len_ref, o_hbm, st_hbm, q_hbm, kv_hbm, dkv_ref, par_ref, path_ref, w_hbm, out_ref, chosen_ref,
-    q_ref, qs_ref, kv_ref, s_ref, peak_ref, o_ref, st_ref, w_ref, pair_o, pair_st, merge_o, merge_st, acc_ref, run_ref, att, rs_send, rs_recv, half_ref,
+    len_ref, q_hbm, kv_hbm, dkv_ref, par_ref, path_ref, w_hbm, out_ref, chosen_ref, kv_ref,
+    q_ref, qs_ref, s_ref, peak_ref, o_ref, st_ref, w_ref, pair_o, pair_st, merge_o, merge_st, acc_ref, run_ref, att, rs_send, rs_recv, half_ref,
     q_sem, qs_sem, kv_sem, in_sem, pair_ss, pair_rs, merge_ss, merge_rs, own_ss, pass_ss, att_rs, out_ss, out_rs, half_sem,
 ):
     s, t = lax.axis_index("seq"), lax.axis_index("tp")
@@ -314,8 +174,8 @@
     pl.semaphore_signal(barrier, inc=1, device_id={"seq": partner}, device_id_type=MESH)
     for d in range(1, tps):
         pl.semaphore_signal(barrier, inc=1, device_id={"tp": (t + d) % tps}, device_id_type=MESH)
-    few, span = o_hbm.shape[0], kv_ref.shape[2]
-    jobs = jnp.where(k < 4, kv_ref.shape[0], kv_ref.shape[0] // 2)
+    span = kv_ref.shape[2]
+    jobs = 4 * sum(jnp.where(k < 2**tenant, 1, 0) for tenant in range(4))
 
     def place(i):
         return 3 - i // 4, i % 4
@@ -343,11 +203,14 @@
         return 0
 
     lax.fori_loop(0, jobs, start_load, 0)
-    w_copy = pltpu.make_async_copy(w_hbm, w_ref, in_sem.at[0])
-    o_copy = pltpu.make_async_copy(o_hbm, o_ref.at[pl.ds(0, few)], in_sem.at[1])
-    st_copy = pltpu.make_async_copy(st_hbm, st_ref.at[pl.ds(0, few)], in_sem.at[2])
-    for copy in (o_copy, st_copy, w_copy):
-        copy.start()
+
+    def start_idle(i, _):
+        kv_load(i).start()
+        return 0
+
+    lax.fori_loop(jobs, kv_ref.shape[0], start_idle, 0)
+    w_copy = pltpu.make_async_copy(w_hbm, w_ref, in_sem)
+    w_copy.start()
 
     def send(src, dst, ss, rs, **where):
         return pltpu.make_async_remote_copy(
@@ -418,6 +281,9 @@
     acc_ref[...] = jnp.dot(dkv_ref[1].T, weights.astype(jnp.bfloat16), preferred_element_type=jnp.float32)
 
     def combine(tenant, turn):
+        pl.when(tenant % 2 == c)(lambda: combine_now(tenant, turn))
+
+    def combine_now(tenant, turn):
         j = 2 * turn + tenant // 2
         r = 4 * tenant + turn
         for copy in pair_copies(j):
@@ -433,17 +299,8 @@
             for copy in merge_copies(j):
                 copy.start()
 
-    def combine_all(tenant):
-        def each(turn, _):
-            combine(tenant, (turn + k // 2) % 4)
-            return 0
-
-        @pl.when((tenant % 2 == c) & (k < 2**tenant))
-        def _():
-            lax.fori_loop(0, 4, each, 0)
-
     def start_pair(tenant, turn):
-        @pl.when((tenant % 2 != c) & (k < reach_of(tenant // 2, tenant % 2)))
+        @pl.when(tenant % 2 != c)
         def _():
             for copy in pair_copies(2 * turn + tenant // 2):
                 copy.start()
@@ -474,12 +331,7 @@
             peak_ref[1 - u : 2 - u] = above
 
     attend_two(0)
-    o_copy.wait()
-    st_copy.wait()
     pl.semaphore_wait(barrier, chips + tps - 1)
-    for tenant in range(2):
-        for turn in range(4):
-            start_pair(tenant, turn)
 
     def start_two(n):
         for u in range(2):
@@ -491,26 +343,13 @@
         attend_two(n)
         start_two(n)
 
-        @pl.when(n == 1)
-        def _():
-            combine_all(0)
-            combine_all(1)
-
-        @pl.when(n == 2)
-        def _():
-            combine_all(3)
-
+        for u in range(2):
+            combine(*place(2 * n - 2 + u))
         return 0
 
     lax.fori_loop(1, jobs // 2, attend_pair, 0)
-
-    @pl.when(k < 4)
-    def _():
-        combine_all(2)
-
-    @pl.when(k >= 4)
-    def _():
-        combine_all(3)
+    for u in range(2):
+        combine(*place(jobs - 2 + u))
 
     def absorb(o, st):
         peak, total, a, b = folded_parts((run_ref[0:1], run_ref[1:2]), (st[0:1], st[1:2]))
@@ -644,14 +483,20 @@
         return 0
 
     lax.fori_loop(0, chips, finish_pair, 0)
+
+    def finish_idle(i, _):
+        kv_load(i).wait()
+        return 0
+
+    lax.fori_loop(jobs, kv_ref.shape[0], finish_idle, 0)
     for copy in own:
         copy.wait_send()
 
 
-def join(lengths, o, st, queries, cache, draft_kv, parents, path, out_weight, chips, tps):
+def join(lengths, queries, cache, draft_kv, parents, path, out_weight, chips, tps):
     requests, span = cache.shape[1], cache.shape[2]
-    few, _, width = o.shape
     wide, columns = queries.shape[1], out_weight.shape[1]
+    width = wide // HEAD * Q
     dma = pltpu.SemaphoreType.DMA
     whole, far = pl.BlockSpec(memory_space=pltpu.VMEM), pl.BlockSpec(memory_space=pl.ANY)
     return pl.pallas_call(
@@ -659,17 +504,17 @@
         out_shape=(
             jax.ShapeDtypeStruct((queries.shape[0] // tps, columns), jnp.bfloat16),
             jax.ShapeDtypeStruct((requests, 4 * ACC, HEAD), jnp.bfloat16),
+            jax.ShapeDtypeStruct((requests, 2, span, HEAD), jnp.bfloat16),
         ),
-        in_specs=[pl.BlockSpec(memory_space=pltpu.SMEM), far, far, far, far, whole, whole, whole, far],
-        out_specs=(whole, whole),
+        in_specs=[pl.BlockSpec(memory_space=pltpu.SMEM), far, far, whole, whole, whole, far],
+        out_specs=(whole, whole, whole),
         scratch_shapes=[
             pltpu.VMEM((Q, wide), jnp.bfloat16),
-            pltpu.VMEM((requests // 2, Q, wide), jnp.bfloat16),
-            pltpu.VMEM((requests // 2, 2, span, HEAD), jnp.bfloat16),
+            pltpu.VMEM((requests, Q, wide), jnp.bfloat16),
             pltpu.VMEM((2, span, width), jnp.float32),
             pltpu.VMEM((8, width), jnp.float32),
-            pltpu.VMEM((requests, HEAD, width), o.dtype),
-            pltpu.VMEM((requests, 8, width), st.dtype),
+            pltpu.VMEM((requests, HEAD, width), jnp.bfloat16),
+            pltpu.VMEM((requests, 8, width), jnp.float32),
             pltpu.VMEM(out_weight.shape, out_weight.dtype),
             pltpu.VMEM((chips, HEAD, width), jnp.bfloat16),
             pltpu.VMEM((chips, 8, width), jnp.float32),
@@ -682,9 +527,9 @@
             pltpu.VMEM((tps, 2 * Q, columns), jnp.bfloat16),
             pltpu.VMEM((2, 2 * Q, columns), jnp.bfloat16),
             dma,
-            dma((requests // 2,)),
-            dma((requests // 2,)),
-            dma((3,)),
+            dma((requests,)),
+            dma((requests,)),
+            dma,
             dma((chips, 2)),
             dma((chips, 2)),
             dma((chips, 2)),
@@ -697,19 +542,18 @@
             dma((2,)),
         ],
         compiler_params=pltpu.CompilerParams(
-            collective_id=0, has_side_effects=True, vmem_limit_bytes=60 << 20
+            collective_id=0, has_side_effects=True, vmem_limit_bytes=40 << 20
         ),
         name="join",
-    )(lengths, o, st, queries, cache, draft_kv, parents, path, out_weight)
+    )(*(pltpu.with_memory_space_constraint(a, pltpu.HBM) for a in (lengths, queries, cache, draft_kv, parents, path, out_weight)))
 
 
 def solution(mesh):
     chips, tps = mesh.shape["seq"] // 2, mesh.shape["tp"]
 
     def local(queries, cache, draft_kv, out_weight, lengths, parents, path, accepted):
-        o, st, new_cache = attend(lengths, queries, cache)
-        attn, chosen = join(lengths, o, st, queries, cache, draft_kv, parents, path.T, out_weight, chips, tps)
-        return commit(lengths, accepted, chosen, attn, new_cache)
+        attn, chosen, held = join(lengths, queries, cache, draft_kv, parents, path.T, out_weight, chips, tps)
+        return commit(lengths, accepted, chosen, attn, held, cache.shape)
 
     return jax.shard_map(
         local,

time: 69 us -> 65.7 us (0.952)
  the two profiles are of different devices: /device:TPU:47 before, /device:TPU:15 now
where the time goes in v6:
time: 65.7 us; the launch traced here: 65.5 us
  Pallas kernels  64.8 us (99%)
  between operations  0.67 us (1%)
    pallas_call x1, Pallas kernels, join(): pl.pallas_call(join_kernel, out_shape=(jax.ShapeDtypeStruct((queries.shap...  59.9 us
    pallas_call x1, Pallas kernels, commit(): pl.pallas_call(commit_kernel, out_shape=(jax.ShapeDtypeStruct(attn.shape,...  4.91 us

profile of v6, /device:TPU:15, one launch (start us, length us, event | category | flops | bytes accessed | tf_op | source)
XLA Modules:
  0.0 65.5 jit_solution(882666043230109926)
XLA Ops:
  0.6 0.0 copy-start
  0.6 0.0 copy-start.1
  0.7 59.9 %join.1 = (bf16[128,512]{1,0:T(8,128)(2,1)S(1)}, bf16[16,32,128]{2,1,0:T(8,128)(2,1)S(1)}, bf16[16,2,1024,128]{3,2,1,0:T(8,128)(2,1)S(1)}) custom-call(s32[16]{0:T(128)} %len_ref.3, bf16[1024,1024]{1,0:T(8,128)(2,1)} %q_hbm.1, bf16[2,16,1024,128]{3,2,1,0:T(8,128)(2,1)} %kv_hbm.1, bf16[2,64,128]{2,1,0:T(8,128)(2,1)} %dkv_ref.1, s32[16,64]{1,0:T(8,128)} %par_ref.1, ...), custom_call_target="tpu_custom_call" | custom-call | tf_op jit(solution)/shard_map/join/pallas_call | solution.py:502
  60.6 0.0 copy-done
  60.6 0.0 copy-done.1
  60.6 4.9 %commit.1 = (bf16[128,512]{1,0:T(8,128)(2,1)}, bf16[2,16,1024,128]{3,2,1,0:T(8,128)(2,1)}) custom-call(s32[16]{0:T(128)S(1)} %copy-done, s32[16]{0:T(128)S(1)} %copy-done.1, bf16[16,32,128]{2,1,0:T(8,128)(2,1)S(1)} %get-tuple-element.5.chosen_ref, bf16[128,512]{1,0:T(8,128)(2,1)S(1)} %get-tuple-element.6.attn_ref, ...), custom_call_target="tpu_custom_call" | custom-call | tf_op jit(solution)/shard_map/commit/pallas_call | solution.py:133
Async XLA Ops:
  0.6 59.9 %copy-start = (s32[16]{0:T(128)S(1)}, s32[16]{0:T(128)}, u32[]{:S(2)}) copy-start(s32[16]{0:T(128)} %len_ref.3) | copy-start | bytes 196
  0.6 59.9 %copy-start.1 = (s32[16]{0:T(128)S(1)}, s32[16]{0:T(128)}, u32[]{:S(2)}) copy-start(s32[16]{0:T(128)} %acc_ref.1) | copy-start | bytes 196

commit v7 on v6

--- a/solution.py
+++ b/solution.py
@@ -246,12 +246,12 @@
         return 2 * ((1 - y) * 4 + (z + d) % 4) + c
 
     def out_copy(g):
-        slot = jnp.where(g % 2 == 1, t, g // 4 * 4 + lx)
-        where = jnp.where(g % 2 == 1, g, t // 4 * 4 + g % 4)
+        slot = jnp.where(g % 2 == 0, t, g // 4 * 4 + lx)
+        where = jnp.where(g % 2 == 0, g, t // 4 * 4 + g % 4)
         return send(rs_send.at[g], rs_recv.at[slot], out_ss.at[g], out_rs.at[slot], tp=where)
 
     def leaves(g):
-        return jnp.where(g % 2 == 1, g != t, g % 4 != lx)
+        return jnp.where(g % 2 == 0, g != t, g % 4 != lx)
 
     def out_arrival(i):
         return send(rs_send.at[i], rs_recv.at[i], out_ss.at[i], out_rs.at[i], seq=partner)
@@ -394,7 +394,7 @@
         copy.start()
 
     def group(i):
-        return (y + i // 2) % 2 * 4 + (z // 2 * 2 + 2 * i + i // 4) % 4
+        return (y + i // 2) % 2 * 4 + (z // 2 * 2 + 2 * i + 1 - i // 4) % 4
 
     def forward(g):
         return pass_on(2 * g + c, pass_ss.at[g], partner)
@@ -447,7 +447,7 @@
 
     swap = send(half_ref.at[0], half_ref.at[1], half_sem.at[0], half_sem.at[1], tp=across)
 
-    @pl.when(t % 2 == 0)
+    @pl.when(t % 2 == 1)
     def _():
         half_ref[0] = gathered(across, row_slots(across)).astype(jnp.bfloat16)
         swap.start()
@@ -455,7 +455,7 @@
         swap.wait()
         out_ref[...] = (total + half_ref[1].astype(jnp.float32)).astype(out_ref.dtype)
 
-    @pl.when(t % 2 == 1)
+    @pl.when(t % 2 == 0)
     def _():
         out_ref[...] = gathered(t, [(t + d) % tps for d in range(1, tps)]).astype(out_ref.dtype)
 

time: 65.7 us -> 62.9 us (0.957)
  the two profiles are of different devices: /device:TPU:15 before, /device:TPU:13 now
where the time goes in v7:
time: 62.9 us; the launch traced here: 62.8 us
  Pallas kernels  62.1 us (99%)
  between operations  0.67 us (1%)
    pallas_call x1, Pallas kernels, join(): pl.pallas_call(join_kernel, out_shape=(jax.ShapeDtypeStruct((queries.shap...  57.2 us
    pallas_call x1, Pallas kernels, commit(): pl.pallas_call(commit_kernel, out_shape=(jax.ShapeDtypeStruct(attn.shape,...  4.91 us

profile of v7, /device:TPU:13, one launch (start us, length us, event | category | flops | bytes accessed | tf_op | source)
XLA Modules:
  0.0 62.8 jit_solution(16288779410340589336)
XLA Ops:
  0.6 0.0 copy-start
  0.6 0.0 copy-start.1
  0.7 57.2 %join.1 = (bf16[128,512]{1,0:T(8,128)(2,1)S(1)}, bf16[16,32,128]{2,1,0:T(8,128)(2,1)S(1)}, bf16[16,2,1024,128]{3,2,1,0:T(8,128)(2,1)S(1)}) custom-call(s32[16]{0:T(128)} %len_ref.3, bf16[1024,1024]{1,0:T(8,128)(2,1)} %q_hbm.1, bf16[2,16,1024,128]{3,2,1,0:T(8,128)(2,1)} %kv_hbm.1, bf16[2,64,128]{2,1,0:T(8,128)(2,1)} %dkv_ref.1, s32[16,64]{1,0:T(8,128)} %par_ref.1, ...), custom_call_target="tpu_custom_call" | custom-call | tf_op jit(solution)/shard_map/join/pallas_call | solution.py:502
  57.8 0.0 copy-done
  57.8 0.0 copy-done.1
  57.8 4.9 %commit.1 = (bf16[128,512]{1,0:T(8,128)(2,1)}, bf16[2,16,1024,128]{3,2,1,0:T(8,128)(2,1)}) custom-call(s32[16]{0:T(128)S(1)} %copy-done, s32[16]{0:T(128)S(1)} %copy-done.1, bf16[16,32,128]{2,1,0:T(8,128)(2,1)S(1)} %get-tuple-element.5.chosen_ref, bf16[128,512]{1,0:T(8,128)(2,1)S(1)} %get-tuple-element.6.attn_ref, ...), custom_call_target="tpu_custom_call" | custom-call | tf_op jit(solution)/shard_map/commit/pallas_call | solution.py:133
Async XLA Ops:
  0.6 57.2 %copy-start = (s32[16]{0:T(128)S(1)}, s32[16]{0:T(128)}, u32[]{:S(2)}) copy-start(s32[16]{0:T(128)} %len_ref.3) | copy-start | bytes 196
  0.6 57.2 %copy-start.1 = (s32[16]{0:T(128)S(1)}, s32[16]{0:T(128)}, u32[]{:S(2)}) copy-start(s32[16]{0:T(128)} %acc_ref.1) | copy-start | bytes 196

commit v8 on v7

--- a/solution.py
+++ b/solution.py
@@ -26,6 +26,8 @@
     s = lax.dot_general(
         kv[0, c * CHUNK : (c + 1) * CHUNK, :], q, (((1,), (1,)), ((), ())), preferred_element_type=jnp.float32
     )
+    if live is None:
+        return s
     row = lax.broadcasted_iota(jnp.int32, s.shape, 0) + c * CHUNK
     return jnp.where(row < live, s, DEAD)
 
@@ -311,43 +313,42 @@
         None, s_ref.at[0], None, kv_ref.at[0], stacked_heads(qs_ref[0]), live(0), s_ref.at[0]
     )
     peak_ref[0:1] = above
-    def attend_two(n):
-        for u in range(2):
-            now = 2 * n + u
-            later = jnp.where(now + 1 < jobs, now + 1, 0)
-
-            @pl.when(now + 1 < jobs)
-            def _():
-                qs_load(later).wait()
-                kv_load(later).wait()
-
-            peak = peak_ref[u : u + 1]
+    def attend_one(n, u, masked=True, ahead=True):
+        now = 2 * n + u
+        peak = peak_ref[u : u + 1]
+        if ahead:
+            later = now + 1
+            qs_load(later).wait()
+            kv_load(later).wait()
             acc, above = attention_step(
                 kv_ref.at[now], s_ref.at[u], peak,
-                kv_ref.at[later], stacked_heads(qs_ref[later]), live(later), s_ref.at[1 - u],
+                kv_ref.at[later], stacked_heads(qs_ref[later]), live(later) if masked else None, s_ref.at[1 - u],
             )
-            tenant, turn = place(now)
-            publish(o_ref.at[4 * tenant + turn], st_ref.at[4 * tenant + turn], peak, acc)
             peak_ref[1 - u : 2 - u] = above
-
-    attend_two(0)
+        else:
+            acc, _ = attention_step(kv_ref.at[now], s_ref.at[u], peak, None, None, None, None)
+        tenant, turn = place(now)
+        publish(o_ref.at[4 * tenant + turn], st_ref.at[4 * tenant + turn], peak, acc)
+
+    for u in range(2):
+        attend_one(0, u)
     pl.semaphore_wait(barrier, chips + tps - 1)
-
-    def start_two(n):
+    for u in range(2):
+        start_pair(*place(u))
+
+    def attend_pair(n, masked=True, last=False):
         for u in range(2):
+            attend_one(n, u, masked, not last or u == 0)
             start_pair(*place(2 * n + u))
-
-    start_two(0)
-
-    def attend_pair(n, _):
-        attend_two(n)
-        start_two(n)
-
         for u in range(2):
             combine(*place(2 * n - 2 + u))
         return 0
 
-    lax.fori_loop(1, jobs // 2, attend_pair, 0)
+    full = 4 * sum(jnp.where(s + 1 < 2**tenant, 1, 0) for tenant in range(4))
+    full, pairs = jnp.maximum(full // 2 - 1, 1), jobs // 2
+    lax.fori_loop(1, full, lambda n, _: attend_pair(n, masked=False), 0)
+    lax.fori_loop(full, pairs - 1, lambda n, _: attend_pair(n), 0)
+    attend_pair(pairs - 1, last=True)
     for u in range(2):
         combine(*place(jobs - 2 + u))
 

time: 62.9 us -> 62.1 us (0.987)
  Pallas kernels: 62.1 us -> 61.3 us
    pallas_call x1, Pallas kernels: 57.2 us -> 56.4 us  [join(): pl.pallas_call(join_kernel, out_shape=(jax.ShapeDtypeStruct((queries.shap...]
where the time goes in v8:
time: 62.1 us; the launch traced here: 61.9 us
  Pallas kernels  61.3 us (99%)
  between operations  0.67 us (1%)
    pallas_call x1, Pallas kernels, join(): pl.pallas_call(join_kernel, out_shape=(jax.ShapeDtypeStruct((queries.shap...  56.4 us
    pallas_call x1, Pallas kernels, commit(): pl.pallas_call(commit_kernel, out_shape=(jax.ShapeDtypeStruct(attn.shape,...  4.91 us

profile of v8, /device:TPU:13, one launch (start us, length us, event | category | flops | bytes accessed | tf_op | source)
XLA Modules:
  0.0 61.9 jit_solution(11713338923337330873)
XLA Ops:
  0.6 0.0 copy-start
  0.6 0.0 copy-start.1
  0.7 56.4 %join.1 = (bf16[128,512]{1,0:T(8,128)(2,1)S(1)}, bf16[16,32,128]{2,1,0:T(8,128)(2,1)S(1)}, bf16[16,2,1024,128]{3,2,1,0:T(8,128)(2,1)S(1)}) custom-call(s32[16]{0:T(128)} %len_ref.3, bf16[1024,1024]{1,0:T(8,128)(2,1)} %q_hbm.1, bf16[2,16,1024,128]{3,2,1,0:T(8,128)(2,1)} %kv_hbm.1, bf16[2,64,128]{2,1,0:T(8,128)(2,1)} %dkv_ref.1, s32[16,64]{1,0:T(8,128)} %par_ref.1, ...), custom_call_target="tpu_custom_call" | custom-call | tf_op jit(solution)/shard_map/join/pallas_call | solution.py:503
  57.0 0.0 copy-done
  57.0 0.0 copy-done.1
  57.0 4.9 %commit.1 = (bf16[128,512]{1,0:T(8,128)(2,1)}, bf16[2,16,1024,128]{3,2,1,0:T(8,128)(2,1)}) custom-call(s32[16]{0:T(128)S(1)} %copy-done, s32[16]{0:T(128)S(1)} %copy-done.1, bf16[16,32,128]{2,1,0:T(8,128)(2,1)S(1)} %get-tuple-element.5.chosen_ref, bf16[128,512]{1,0:T(8,128)(2,1)S(1)} %get-tuple-element.6.attn_ref, ...), custom_call_target="tpu_custom_call" | custom-call | tf_op jit(solution)/shard_map/commit/pallas_call | solution.py:135
Async XLA Ops:
  0.6 56.4 %copy-start = (s32[16]{0:T(128)S(1)}, s32[16]{0:T(128)}, u32[]{:S(2)}) copy-start(s32[16]{0:T(128)} %len_ref.3) | copy-start | bytes 196
  0.6 56.4 %copy-start.1 = (s32[16]{0:T(128)S(1)}, s32[16]{0:T(128)}, u32[]{:S(2)}) copy-start(s32[16]{0:T(128)} %acc_ref.1) | copy-start | bytes 196
